TPU v7x, 256 devices: a whole 4x4x8 slice. The times are simulated.
256 devices in a mesh: gx: 32 (over z, x), gy: 8 (over y, core).
Axes of the slice: x: 4, y: 4, z: 8, core: 2. Of those that a mesh axis runs over, the one named last changes fastest.
Arguments:
- velocity: float32 [1, 2048, 2048], P(None, 'gx', 'gy'), may hold values from -6 to 6
Outputs:
- du_dx: float32 [1, 2048, 2048], P(None, 'gx', 'gy')
- du_dy: float32 [1, 2048, 2048], P(None, 'gx', 'gy')
- d2u_dx2: float32 [1, 2048, 2048], P(None, 'gx', 'gy')
- d2u_dy2: float32 [1, 2048, 2048], P(None, 'gx', 'gy')
All inputs are finite; a program needn't handle non-finite values.
Results may differ from a plain program's by a relative error of at most 0.00007.
Values sent between devices are 32-bit elements; how exact they have to be, the bound alone decides.
A program may use at most 64 MiB of HBM per device.

v0:
```python
import jax
import jax.numpy as jnp
from jax import lax
from jax.sharding import PartitionSpec as P

FIRST_NEAR = 7.0 / 9.0
FIRST_FAR = 1.0 / 36.0
SECOND_NEAR = 12.0 / 11.0
SECOND_FAR = 3.0 / 44.0
COUPLINGS = (1.0 / 3.0, 2.0 / 11.0)
HIGHEST = lax.Precision.HIGHEST
window_margin = 24


def stencils(shifted):
    minus_two, minus_one, centre, plus_one, plus_two = shifted
    first_order = FIRST_NEAR * (plus_one - minus_one) + FIRST_FAR * (plus_two - minus_two)
    second_order = SECOND_NEAR * (plus_one - 2.0 * centre + minus_one) + SECOND_FAR * (
        plus_two - 2.0 * centre + minus_two
    )
    return jnp.stack([first_order, second_order])


def window_rows(coupling, block):
    length = block + 2 * window_margin
    coupled = jnp.full((length - 1,), coupling, jnp.float32)
    zero_entry = jnp.zeros((1,), jnp.float32)
    lower = jnp.concatenate([zero_entry, coupled])
    upper = jnp.concatenate([coupled, zero_entry])
    diagonal = jnp.ones((length,), jnp.float32)
    inverse = lax.linalg.tridiagonal_solve(
        lower, diagonal, upper, jnp.eye(length, dtype=jnp.float32)
    )
    return inverse[window_margin : window_margin + block]


def window_stack(block):
    return jnp.stack([window_rows(coupling, block) for coupling in COUPLINGS])


def line_stencils(lines):
    return stencils([jnp.roll(lines, 2 - k, axis=-1) for k in range(5)])


def windowed_solve(sources, matrices, block):
    leading = sources.shape[:-1]
    count = sources.shape[-1] // block
    blocks = sources.reshape(leading + (count, block))
    left_part = jnp.roll(blocks, 1, axis=-2)[..., block - window_margin :]
    right_part = jnp.roll(blocks, -1, axis=-2)[..., :window_margin]
    extended = jnp.concatenate([left_part, blocks, right_part], axis=-1)
    solved = jnp.einsum("sij,spqbj->spqbi", matrices, extended, precision=HIGHEST)
    return solved.reshape(sources.shape)


def local(velocity):
    cells_x = velocity.shape[1]
    cells_y = velocity.shape[2]
    matrices_x = window_stack(cells_x)
    matrices_y = window_stack(cells_y)
    turned = jnp.swapaxes(velocity, 1, 2)
    solved = windowed_solve(
        line_stencils(lax.all_to_all(turned, "gx", split_axis=1, concat_axis=2, tiled=True)),
        matrices_x,
        cells_x,
    )
    solved_x = lax.all_to_all(solved, "gx", split_axis=3, concat_axis=2, tiled=True)
    solved_x = jnp.swapaxes(solved_x, 2, 3)
    solved = windowed_solve(
        line_stencils(lax.all_to_all(velocity, "gy", split_axis=1, concat_axis=2, tiled=True)),
        matrices_y,
        cells_y,
    )
    solved_y = lax.all_to_all(solved, "gy", split_axis=3, concat_axis=2, tiled=True)
    return (solved_x[0], solved_y[0], solved_x[1], solved_y[1])


def solution(mesh):
    placed = (P(None, "gx", "gy"),)
    return jax.shard_map(
        local,
        mesh=mesh,
        in_specs=placed,
        out_specs=(
            P(None, "gx", "gy"),
            P(None, "gx", "gy"),
            P(None, "gx", "gy"),
            P(None, "gx", "gy"),
        ),
        check_vma=False,
    )
```

profile of v0, /device:TPU:8, one launch (start us, length us, event | category | flops | bytes accessed | tf_op | source)
XLA Modules:
  0.0 671.2 jit_solution(12084022380774429123)
XLA Ops:
  0.6 1.5 copy.87
  2.2 5.4 all-to-all-start.2
  8.8 24.0 %while.132 = (s32[]{:T(128)}, f32[]{:T(128)}, f32[304]{0:T(512)S(1)}, f32[9,32]{1,0:T(8,128)S(1)}, f32[9,32,304]{2,1,0:T(8,128)S(1)}, /*index=5*/f32[9,32,304]{2...) while((s32[]{:T(128)}, f32[]{:T(128)}, ...), condition=%wide.region_9.10_spmd, body=%wide.region_8.9_spmd.sunk | while | flops 29313 | bytes 413469 | solution.py:31
  34.3 201.8 %while.133 = (s32[]{:T(128)}, f32[304]{0:T(512)S(1)}, f32[9,32,304]{2,1,0:T(8,128)S(1)}, f32[9,32,304]{2,1,0:T(8,128)S(1)}, f32[9,32]{1,0:T(8,128)S(1)}, /*index...) while((s32[]{:T(128)}, f32[304]{0:T(512)S(1)}, ...), condition=%wide.region_11.12_spmd, body=%wide.region_10.11_spmd.sunk | while | flops 19490 | bytes 412313 | solution.py:31
  36.0 20.2 %multiply_subtract_fusion.128 = (f32[304]{0:T(512)S(1)}, f32[304]{0:T(512)S(1)}, f32[304]{0:T(512)S(1)}, f32[304]{0:T(512)S(1)}, f32[304]{0:T(512)S(1)}, /*index...) fusion(f32[304]{0:T(512)S(1)} %get-tuple-element.2331, ...), kind=kLoop, calls=%fused_computation.585.clone.1 | loop fusion | flops 19456 | bytes 79168 | tf_op jit(solution)/shard_map/while/body/eval_jaxpr/sub | solution.py:31
  58.4 20.2 %multiply_subtract_fusion.128 = (f32[304]{0:T(512)S(1)}, f32[304]{0:T(512)S(1)}, f32[304]{0:T(512)S(1)}, f32[304]{0:T(512)S(1)}, f32[304]{0:T(512)S(1)}, /*index...) fusion(f32[304]{0:T(512)S(1)} %get-tuple-element.2331, ...), kind=kLoop, calls=%fused_computation.585.clone.1 | loop fusion | flops 19456 | bytes 79168 | tf_op jit(solution)/shard_map/while/body/eval_jaxpr/sub | solution.py:31
  80.9 20.2 %multiply_subtract_fusion.128 = (f32[304]{0:T(512)S(1)}, f32[304]{0:T(512)S(1)}, f32[304]{0:T(512)S(1)}, f32[304]{0:T(512)S(1)}, f32[304]{0:T(512)S(1)}, /*index...) fusion(f32[304]{0:T(512)S(1)} %get-tuple-element.2331, ...), kind=kLoop, calls=%fused_computation.585.clone.1 | loop fusion | flops 19456 | bytes 79168 | tf_op jit(solution)/shard_map/while/body/eval_jaxpr/sub | solution.py:31
  103.3 20.2 %multiply_subtract_fusion.128 = (f32[304]{0:T(512)S(1)}, f32[304]{0:T(512)S(1)}, f32[304]{0:T(512)S(1)}, f32[304]{0:T(512)S(1)}, f32[304]{0:T(512)S(1)}, /*index...) fusion(f32[304]{0:T(512)S(1)} %get-tuple-element.2331, ...), kind=kLoop, calls=%fused_computation.585.clone.1 | loop fusion | flops 19456 | bytes 79168 | tf_op jit(solution)/shard_map/while/body/eval_jaxpr/sub | solution.py:31
  125.7 20.2 %multiply_subtract_fusion.128 = (f32[304]{0:T(512)S(1)}, f32[304]{0:T(512)S(1)}, f32[304]{0:T(512)S(1)}, f32[304]{0:T(512)S(1)}, f32[304]{0:T(512)S(1)}, /*index...) fusion(f32[304]{0:T(512)S(1)} %get-tuple-element.2331, ...), kind=kLoop, calls=%fused_computation.585.clone.1 | loop fusion | flops 19456 | bytes 79168 | tf_op jit(solution)/shard_map/while/body/eval_jaxpr/sub | solution.py:31
  148.1 20.2 %multiply_subtract_fusion.128 = (f32[304]{0:T(512)S(1)}, f32[304]{0:T(512)S(1)}, f32[304]{0:T(512)S(1)}, f32[304]{0:T(512)S(1)}, f32[304]{0:T(512)S(1)}, /*index...) fusion(f32[304]{0:T(512)S(1)} %get-tuple-element.2331, ...), kind=kLoop, calls=%fused_computation.585.clone.1 | loop fusion | flops 19456 | bytes 79168 | tf_op jit(solution)/shard_map/while/body/eval_jaxpr/sub | solution.py:31
  170.5 20.2 %multiply_subtract_fusion.128 = (f32[304]{0:T(512)S(1)}, f32[304]{0:T(512)S(1)}, f32[304]{0:T(512)S(1)}, f32[304]{0:T(512)S(1)}, f32[304]{0:T(512)S(1)}, /*index...) fusion(f32[304]{0:T(512)S(1)} %get-tuple-element.2331, ...), kind=kLoop, calls=%fused_computation.585.clone.1 | loop fusion | flops 19456 | bytes 79168 | tf_op jit(solution)/shard_map/while/body/eval_jaxpr/sub | solution.py:31
  193.0 20.2 %multiply_subtract_fusion.128 = (f32[304]{0:T(512)S(1)}, f32[304]{0:T(512)S(1)}, f32[304]{0:T(512)S(1)}, f32[304]{0:T(512)S(1)}, f32[304]{0:T(512)S(1)}, /*index...) fusion(f32[304]{0:T(512)S(1)} %get-tuple-element.2331, ...), kind=kLoop, calls=%fused_computation.585.clone.1 | loop fusion | flops 19456 | bytes 79168 | tf_op jit(solution)/shard_map/while/body/eval_jaxpr/sub | solution.py:31
  215.4 20.2 %multiply_subtract_fusion.128 = (f32[304]{0:T(512)S(1)}, f32[304]{0:T(512)S(1)}, f32[304]{0:T(512)S(1)}, f32[304]{0:T(512)S(1)}, f32[304]{0:T(512)S(1)}, /*index...) fusion(f32[304]{0:T(512)S(1)} %get-tuple-element.2331, ...), kind=kLoop, calls=%fused_computation.585.clone.1 | loop fusion | flops 19456 | bytes 79168 | tf_op jit(solution)/shard_map/while/body/eval_jaxpr/sub | solution.py:31
  236.1 24.0 %while.134 = (s32[]{:T(128)}, f32[]{:T(128)}, f32[304]{0:T(512)S(1)}, f32[9,32]{1,0:T(8,128)S(1)}, f32[9,32,304]{2,1,0:T(8,128)S(1)}, /*index=5*/f32[9,32,304]{2...) while((s32[]{:T(128)}, f32[]{:T(128)}, ...), condition=%wide.region_13.14_spmd, body=%wide.region_12.13_spmd.sunk | while | flops 29313 | bytes 413469 | solution.py:31
  261.6 201.5 %while.135 = (s32[]{:T(128)}, f32[304]{0:T(512)S(1)}, f32[9,32,304]{2,1,0:T(8,128)S(1)}, f32[9,32,304]{2,1,0:T(8,128)S(1)}, f32[9,32]{1,0:T(8,128)S(1)}, /*index...) while((s32[]{:T(128)}, f32[304]{0:T(512)S(1)}, ...), condition=%wide.region_15.16_spmd, body=%wide.region_14.15_spmd.sunk | while | flops 19490 | bytes 412313 | solution.py:31
  263.4 20.1 %multiply_subtract_fusion.129 = (f32[304]{0:T(512)S(1)}, f32[304]{0:T(512)S(1)}, f32[304]{0:T(512)S(1)}, f32[304]{0:T(512)S(1)}, f32[304]{0:T(512)S(1)}, /*index...) fusion(f32[304]{0:T(512)S(1)} %get-tuple-element.2502, ...), kind=kLoop, calls=%fused_computation.780.clone.1 | loop fusion | flops 19456 | bytes 79168 | tf_op jit(solution)/shard_map/while/body/eval_jaxpr/sub | solution.py:31
  285.8 20.1 %multiply_subtract_fusion.129 = (f32[304]{0:T(512)S(1)}, f32[304]{0:T(512)S(1)}, f32[304]{0:T(512)S(1)}, f32[304]{0:T(512)S(1)}, f32[304]{0:T(512)S(1)}, /*index...) fusion(f32[304]{0:T(512)S(1)} %get-tuple-element.2502, ...), kind=kLoop, calls=%fused_computation.780.clone.1 | loop fusion | flops 19456 | bytes 79168 | tf_op jit(solution)/shard_map/while/body/eval_jaxpr/sub | solution.py:31
  308.2 20.1 %multiply_subtract_fusion.129 = (f32[304]{0:T(512)S(1)}, f32[304]{0:T(512)S(1)}, f32[304]{0:T(512)S(1)}, f32[304]{0:T(512)S(1)}, f32[304]{0:T(512)S(1)}, /*index...) fusion(f32[304]{0:T(512)S(1)} %get-tuple-element.2502, ...), kind=kLoop, calls=%fused_computation.780.clone.1 | loop fusion | flops 19456 | bytes 79168 | tf_op jit(solution)/shard_map/while/body/eval_jaxpr/sub | solution.py:31
  330.5 20.1 %multiply_subtract_fusion.129 = (f32[304]{0:T(512)S(1)}, f32[304]{0:T(512)S(1)}, f32[304]{0:T(512)S(1)}, f32[304]{0:T(512)S(1)}, f32[304]{0:T(512)S(1)}, /*index...) fusion(f32[304]{0:T(512)S(1)} %get-tuple-element.2502, ...), kind=kLoop, calls=%fused_computation.780.clone.1 | loop fusion | flops 19456 | bytes 79168 | tf_op jit(solution)/shard_map/while/body/eval_jaxpr/sub | solution.py:31
  352.9 20.1 %multiply_subtract_fusion.129 = (f32[304]{0:T(512)S(1)}, f32[304]{0:T(512)S(1)}, f32[304]{0:T(512)S(1)}, f32[304]{0:T(512)S(1)}, f32[304]{0:T(512)S(1)}, /*index...) fusion(f32[304]{0:T(512)S(1)} %get-tuple-element.2502, ...), kind=kLoop, calls=%fused_computation.780.clone.1 | loop fusion | flops 19456 | bytes 79168 | tf_op jit(solution)/shard_map/while/body/eval_jaxpr/sub | solution.py:31
  375.3 20.1 %multiply_subtract_fusion.129 = (f32[304]{0:T(512)S(1)}, f32[304]{0:T(512)S(1)}, f32[304]{0:T(512)S(1)}, f32[304]{0:T(512)S(1)}, f32[304]{0:T(512)S(1)}, /*index...) fusion(f32[304]{0:T(512)S(1)} %get-tuple-element.2502, ...), kind=kLoop, calls=%fused_computation.780.clone.1 | loop fusion | flops 19456 | bytes 79168 | tf_op jit(solution)/shard_map/while/body/eval_jaxpr/sub | solution.py:31
  397.7 20.1 %multiply_subtract_fusion.129 = (f32[304]{0:T(512)S(1)}, f32[304]{0:T(512)S(1)}, f32[304]{0:T(512)S(1)}, f32[304]{0:T(512)S(1)}, f32[304]{0:T(512)S(1)}, /*index...) fusion(f32[304]{0:T(512)S(1)} %get-tuple-element.2502, ...), kind=kLoop, calls=%fused_computation.780.clone.1 | loop fusion | flops 19456 | bytes 79168 | tf_op jit(solution)/shard_map/while/body/eval_jaxpr/sub | solution.py:31
  420.1 20.1 %multiply_subtract_fusion.129 = (f32[304]{0:T(512)S(1)}, f32[304]{0:T(512)S(1)}, f32[304]{0:T(512)S(1)}, f32[304]{0:T(512)S(1)}, f32[304]{0:T(512)S(1)}, /*index...) fusion(f32[304]{0:T(512)S(1)} %get-tuple-element.2502, ...), kind=kLoop, calls=%fused_computation.780.clone.1 | loop fusion | flops 19456 | bytes 79168 | tf_op jit(solution)/shard_map/while/body/eval_jaxpr/sub | solution.py:31
  442.5 20.1 %multiply_subtract_fusion.129 = (f32[304]{0:T(512)S(1)}, f32[304]{0:T(512)S(1)}, f32[304]{0:T(512)S(1)}, f32[304]{0:T(512)S(1)}, f32[304]{0:T(512)S(1)}, /*index...) fusion(f32[304]{0:T(512)S(1)} %get-tuple-element.2502, ...), kind=kLoop, calls=%fused_computation.780.clone.1 | loop fusion | flops 19456 | bytes 79168 | tf_op jit(solution)/shard_map/while/body/eval_jaxpr/sub | solution.py:31
  463.2 5.9 while.128
  470.1 65.4 %while.129 = (s32[]{:T(128)}, f32[112]{0:T(128)S(1)}, f32[3,32,112]{2,1,0:T(8,128)S(1)}, f32[3,32,112]{2,1,0:T(8,128)S(1)}, f32[3,32]{1,0:T(4,128)S(1)}, /*index...) while((s32[]{:T(128)}, f32[112]{0:T(128)S(1)}, ...), condition=%wide.region_3.4_spmd, body=%wide.region_2.3_spmd.sunk | while | flops 7202 | bytes 92949 | solution.py:31
  471.6 20.2 %fusion.653 = (f32[112]{0:T(128)S(1)}, f32[112]{0:T(128)S(1)}, f32[112]{0:T(128)S(1)}, f32[112]{0:T(128)S(1)}, f32[112]{0:T(128)S(1)}, /*index=5*/f32[112]{0:T(1...) fusion(f32[3,32,112]{2,1,0:T(8,128)S(1)} %get-tuple-element.304, ...), kind=kLoop, calls=%fused_computation.166.clone.1 | loop fusion | flops 7168 | bytes 29376 | tf_op jit(solution)/shard_map/while/body/eval_jaxpr/sub | solution.py:31
  493.4 20.2 %fusion.653 = (f32[112]{0:T(128)S(1)}, f32[112]{0:T(128)S(1)}, f32[112]{0:T(128)S(1)}, f32[112]{0:T(128)S(1)}, f32[112]{0:T(128)S(1)}, /*index=5*/f32[112]{0:T(1...) fusion(f32[3,32,112]{2,1,0:T(8,128)S(1)} %get-tuple-element.304, ...), kind=kLoop, calls=%fused_computation.166.clone.1 | loop fusion | flops 7168 | bytes 29376 | tf_op jit(solution)/shard_map/while/body/eval_jaxpr/sub | solution.py:31
  515.2 20.2 %fusion.653 = (f32[112]{0:T(128)S(1)}, f32[112]{0:T(128)S(1)}, f32[112]{0:T(128)S(1)}, f32[112]{0:T(128)S(1)}, f32[112]{0:T(128)S(1)}, /*index=5*/f32[112]{0:T(1...) fusion(f32[3,32,112]{2,1,0:T(8,128)S(1)} %get-tuple-element.304, ...), kind=kLoop, calls=%fused_computation.166.clone.1 | loop fusion | flops 7168 | bytes 29376 | tf_op jit(solution)/shard_map/while/body/eval_jaxpr/sub | solution.py:31
  535.6 5.9 while.130
  542.6 65.6 %while.131 = (s32[]{:T(128)}, f32[112]{0:T(128)S(1)}, f32[3,32,112]{2,1,0:T(8,128)S(1)}, f32[3,32,112]{2,1,0:T(8,128)S(1)}, f32[3,32]{1,0:T(4,128)S(1)}, /*index...) while((s32[]{:T(128)}, f32[112]{0:T(128)S(1)}, ...), condition=%wide.region_7.8_spmd, body=%wide.region_6.7_spmd.sunk | while | flops 7202 | bytes 92949 | solution.py:31
  544.0 20.3 %fusion.657 = (f32[112]{0:T(128)S(1)}, f32[112]{0:T(128)S(1)}, f32[112]{0:T(128)S(1)}, f32[112]{0:T(128)S(1)}, f32[112]{0:T(128)S(1)}, /*index=5*/f32[112]{0:T(1...) fusion(f32[3,32,112]{2,1,0:T(8,128)S(1)} %get-tuple-element.280, ...), kind=kLoop, calls=%fused_computation.393.clone.1 | loop fusion | flops 7168 | bytes 29376 | tf_op jit(solution)/shard_map/while/body/eval_jaxpr/sub | solution.py:31
  565.9 20.3 %fusion.657 = (f32[112]{0:T(128)S(1)}, f32[112]{0:T(128)S(1)}, f32[112]{0:T(128)S(1)}, f32[112]{0:T(128)S(1)}, f32[112]{0:T(128)S(1)}, /*index=5*/f32[112]{0:T(1...) fusion(f32[3,32,112]{2,1,0:T(8,128)S(1)} %get-tuple-element.280, ...), kind=kLoop, calls=%fused_computation.393.clone.1 | loop fusion | flops 7168 | bytes 29376 | tf_op jit(solution)/shard_map/while/body/eval_jaxpr/sub | solution.py:31
  587.8 20.3 %fusion.657 = (f32[112]{0:T(128)S(1)}, f32[112]{0:T(128)S(1)}, f32[112]{0:T(128)S(1)}, f32[112]{0:T(128)S(1)}, f32[112]{0:T(128)S(1)}, /*index=5*/f32[112]{0:T(1...) fusion(f32[3,32,112]{2,1,0:T(8,128)S(1)} %get-tuple-element.280, ...), kind=kLoop, calls=%fused_computation.393.clone.1 | loop fusion | flops 7168 | bytes 29376 | tf_op jit(solution)/shard_map/while/body/eval_jaxpr/sub | solution.py:31
  609.1 1.0 reduce.288
  610.8 11.0 %all-to-all-start = ((f32[32,1,512]{2,1,0:T(1,128)}), f32[32,1,512]{2,1,0:T(1,128)S(1)}, u32[]{:S(2)}, u32[]{:S(2)}) async-start(f32[32,1,512]{2,1,0:T(1,128)} %reshape.1462), calls=%async_computation | async-start | bytes 131072 | tf_op jit(solution)/shard_map/all_to_all | solution.py:63
  624.8 4.0 reshape.1466
  628.7 2.9 all-to-all-done
  631.6 4.8 all-to-all-start.3
  639.8 1.1 copy.106
  640.9 4.0 reshape.1464
  644.9 6.9 %all-to-all-start.1 = ((f32[32,1,1024]{2,1,0:T(1,128)}), f32[32,1,1024]{2,1,0:T(1,128)S(1)}, u32[]{:S(2)}, u32[]{:S(2)}) async-start(f32[32,1,1024]{2,1,0:T(1,128)} %reshape.1464), calls=%async_computation.1 | async-start | bytes 262144 | tf_op jit(solution)/shard_map/all_to_all | solution.py:67
  652.8 3.2 reshape.1467
  656.0 3.0 fusion.625
  659.0 3.3 copy.100
  662.4 1.6 copy.101
  664.9 3.2 reshape.1465
  668.1 1.7 copy.108
  (1622 shorter events, 79.8 us)
Async XLA Ops:
  2.2 608.7 %all-to-all-start.2 = ((f32[1,64,256]{2,0,1:T(1,128)}), f32[1,64,256]{2,0,1:T(1,128)S(1)}, u32[]{:S(2)}, u32[]{:S(2)}) async-start(f32[1,64,256]{2,0,1:T(1,128)} %copy.87), calls=%async_computation.2 | async-start | bytes 131072 | tf_op jit(solution)/shard_map/all_to_all | solution.py:70
  7.8 1.0 copy-start
  261.6 201.6 %copy-start.2 = (f32[112]{0:T(128)S(1)}, f32[112]{0:T(128)}, u32[]{:S(2)}) copy-start(f32[112]{0:T(128)} %copy-done) | copy-start | bytes 1348
  469.0 66.6 %copy-start.1 = (f32[112]{0:T(128)S(1)}, f32[112]{0:T(128)}, u32[]{:S(2)}) copy-start(f32[112]{0:T(128)} %copy-done) | copy-start | bytes 1348
  610.8 20.8 %all-to-all-start = ((f32[32,1,512]{2,1,0:T(1,128)}), f32[32,1,512]{2,1,0:T(1,128)S(1)}, u32[]{:S(2)}, u32[]{:S(2)}) async-start(f32[32,1,512]{2,1,0:T(1,128)} %reshape.1462), calls=%async_computation | async-start | bytes 131072 | tf_op jit(solution)/shard_map/all_to_all | solution.py:63
  631.6 13.3 %all-to-all-start.3 = ((f32[8,1,4096]{2,1,0:T(1,128)}), f32[8,1,4096]{2,1,0:T(1,128)S(1)}, u32[]{:S(2)}, u32[]{:S(2)}) async-start(f32[8,1,4096]{2,1,0:T(1,128)} %reshape.1466), calls=%async_computation.3 | async-start | bytes 262144 | tf_op jit(solution)/shard_map/all_to_all | solution.py:74
  644.9 19.0 %all-to-all-start.1 = ((f32[32,1,1024]{2,1,0:T(1,128)}), f32[32,1,1024]{2,1,0:T(1,128)S(1)}, u32[]{:S(2)}, u32[]{:S(2)}) async-start(f32[32,1,1024]{2,1,0:T(1,128)} %reshape.1464), calls=%async_computation.1 | async-start | bytes 262144 | tf_op jit(solution)/shard_map/all_to_all | solution.py:67
where the time goes:
time: 679 us; the launch traced here: 671 us
  other arithmetic  496 us (73%)
  local copies, waits for them, and re-layouts  94.6 us (14%)
  loops' own time  44.5 us (7%)
  starting transfers between devices  28.2 us (4%)
    sub x24, other arithmetic, window_rows(): lax.linalg.tridiagonal_solve(lower, diagonal, upper, jnp.eye(length, dtyp...  485 us
    slice x131, local copies, waits for them, and re-layouts, window_rows(): lax.linalg.tridiagonal_solve(lower, diagonal, upper, jnp.eye(length, dtyp...  45.1 us
    another operation x8, loops' own time, window_rows(): lax.linalg.tridiagonal_solve(lower, diagonal, upper, jnp.eye(length, dtyp...  44.5 us
    unnamed x30, local copies, waits for them, and re-layouts  20.6 us
  transfers between devices with their start and end apart: 4, of which 1 were waited for; matrix products, arithmetic and copies ran while one was open for 87% of the time, Pallas kernels for 0%

commit v1 on v0

v1 whole, which is shorter than its diff:
```python
import functools
import math

import jax
import jax.numpy as jnp
from jax import lax
from jax.experimental import pallas as pl
from jax.experimental.pallas import tpu as pltpu
from jax.sharding import PartitionSpec as P

FIRST_NEAR = 7.0 / 9.0
FIRST_FAR = 1.0 / 36.0
SECOND_NEAR = 12.0 / 11.0
SECOND_FAR = 3.0 / 44.0
COUPLINGS = (1.0 / 3.0, 2.0 / 11.0)
MESH = pl.DeviceIdType.MESH
HALO = 24
F32 = jnp.float32
BF16 = jnp.bfloat16


def green(coupling):
    root = math.sqrt(1.0 - 4.0 * coupling * coupling)
    return (1.0 - root) / (2.0 * coupling), 1.0 / root


def powers(coupling, distance):
    ratio, scale = green(coupling)
    size = scale * jnp.exp(distance.astype(F32) * math.log(ratio))
    return jnp.where(distance % 2 == 0, size, -size)


def stencils(u, axis):
    n = u.shape[axis]
    plus_one = pltpu.roll(u, n - 1, axis)
    minus_one = pltpu.roll(u, 1, axis)
    plus_two = pltpu.roll(u, n - 2, axis)
    minus_two = pltpu.roll(u, 2, axis)
    first = FIRST_NEAR * (plus_one - minus_one) + FIRST_FAR * (plus_two - minus_two)
    second = SECOND_NEAR * (plus_one - 2.0 * u + minus_one) + SECOND_FAR * (
        plus_two - 2.0 * u + minus_two
    )
    return first, second


def iota(shape, axis):
    return lax.broadcasted_iota(jnp.int32, shape, axis)


def split(a):
    high = a.astype(BF16)
    return high, (a - high.astype(F32)).astype(BF16)


def dot(a, b):
    return jnp.dot(a, b, preferred_element_type=F32)


def dot3(a, b):
    ah, al = split(a)
    bh, bl = split(b)
    return dot(ah, bh) + dot(al, bh) + dot(ah, bl)


def kernel(nx, ny, v_ref, dx_ref, dy_ref, dxx_ref, dyy_ref, u_ref, xl, xr, yl, yr, local_sem, send, recv):
    ix = lax.axis_index("gx")
    iy = lax.axis_index("gy")
    up = {"gx": lax.rem(ix + 1, nx)}
    down = {"gx": lax.rem(ix + nx - 1, nx)}
    right = {"gy": lax.rem(iy + 1, ny)}
    left = {"gy": lax.rem(iy + ny - 1, ny)}
    rows, cols = u_ref.shape

    load = pltpu.make_async_copy(v_ref.at[0], u_ref, local_sem)
    load.start()
    barrier = pltpu.get_barrier_semaphore()
    for other in (up, down, left, right):
        pl.semaphore_signal(barrier, inc=1, device_id=other, device_id_type=MESH)
    load.wait()
    pl.semaphore_wait(barrier, 4)

    copies = []
    for k, (src, dst, other) in enumerate(
        (
            (u_ref.at[pl.ds(rows - HALO, HALO), :], xl, up),
            (u_ref.at[pl.ds(0, HALO), :], xr, down),
            (u_ref.at[:, pl.ds(cols - 128, 128)], yl, right),
            (u_ref.at[:, pl.ds(0, 128)], yr, left),
        )
    ):
        copy = pltpu.make_async_remote_copy(
            src_ref=src,
            dst_ref=dst,
            send_sem=send.at[k],
            recv_sem=recv.at[k],
            device_id=other,
            device_id_type=MESH,
        )
        copy.start()
        copies.append(copy)

    u = u_ref[...]
    row = iota((rows, cols), 0)
    col = iota((rows, cols), 1)
    inner = (row >= 2) & (row < rows - 2)
    rx = [jnp.where(inner, s, 0.0) for s in stencils(u, 0)]
    distance = jnp.abs(iota((rows, rows), 0) - iota((rows, rows), 1))
    fx = [dot3(powers(c, distance), s) for c, s in zip(COUPLINGS, rx)]
    inner = (col >= 2) & (col < cols - 2)
    ry = [jnp.where(inner, s, 0.0) for s in stencils(u, 1)]
    distance = jnp.abs(iota((cols, cols), 0) - iota((cols, cols), 1))
    fy = [dot3(s, powers(c, distance)) for c, s in zip(COUPLINGS, ry)]

    for copy in copies:
        copy.wait_recv()

    edge = HALO + 8
    place = iota((edge, cols), 0)
    lower = stencils(jnp.concatenate([xl[...], u[:8]], axis=0), 0)
    upper = stencils(jnp.concatenate([u[rows - 8 :], xr[...]], axis=0), 0)
    for k, c in enumerate(COUPLINGS):
        _, scale = green(c)
        weight = jnp.where((place >= 2) & (place <= HALO), powers(c, jnp.abs(HALO - place)), 0.0)
        total = jnp.sum(weight * lower[k], axis=0, keepdims=True) / scale
        fx[k] += powers(c, row) * total + powers(c, jnp.abs(row - 1)) * lower[k][HALO + 1 : HALO + 2]
        weight = jnp.where((place >= 7) & (place < edge - 2), powers(c, jnp.abs(place - 7)), 0.0)
        total = jnp.sum(weight * upper[k], axis=0, keepdims=True) / scale
        fx[k] += (
            powers(c, rows - 1 - row) * total
            + powers(c, jnp.abs(rows - 2 - row)) * upper[k][6:7]
        )

    lane = iota((rows, 128), 1)
    lower = stencils(
        jnp.where(lane < 64, pltpu.roll(yl[...], 64, 1), pltpu.roll(u[:, :128], 64, 1)), 1
    )
    upper = stencils(
        jnp.where(lane < 64, pltpu.roll(u[:, cols - 128 :], 64, 1), pltpu.roll(yr[...], 64, 1)), 1
    )
    source = iota((128, 128), 0)
    target = iota((128, 128), 1)
    sides = [[], []]
    for k, c in enumerate(COUPLINGS):
        low = jnp.where((lane >= 2) & (lane < 66), lower[k], 0.0)
        sides[k].append(dot3(low, powers(c, jnp.abs(target - (source - 64)))))
        high = jnp.where((lane >= 62) & (lane < 126), upper[k], 0.0)
        sides[k].append(dot3(high, powers(c, jnp.abs(target - (source + 64)))))
        fy[k] += jnp.concatenate(sides[k], axis=1)

    dx_ref[0] = fx[0]
    dxx_ref[0] = fx[1]
    dy_ref[0] = fy[0]
    dyy_ref[0] = fy[1]
    for copy in copies:
        copy.wait_send()


def local(nx, ny, velocity):
    _, rows, cols = velocity.shape
    out = jax.ShapeDtypeStruct(velocity.shape, F32)
    return pl.pallas_call(
        functools.partial(kernel, nx, ny),
        out_shape=(out,) * 4,
        in_specs=[pl.BlockSpec(memory_space=pl.ANY)],
        out_specs=[pl.BlockSpec(memory_space=pltpu.VMEM)] * 4,
        scratch_shapes=[
            pltpu.VMEM((rows, cols), F32),
            pltpu.VMEM((HALO, cols), F32),
            pltpu.VMEM((HALO, cols), F32),
            pltpu.VMEM((rows, 128), F32),
            pltpu.VMEM((rows, 128), F32),
            pltpu.SemaphoreType.DMA,
            pltpu.SemaphoreType.DMA((4,)),
            pltpu.SemaphoreType.DMA((4,)),
        ],
        compiler_params=pltpu.CompilerParams(collective_id=0, has_side_effects=True),
    )(velocity)


def solution(mesh):
    placed = P(None, "gx", "gy")
    return jax.shard_map(
        functools.partial(local, mesh.shape["gx"], mesh.shape["gy"]),
        mesh=mesh,
        in_specs=(placed,),
        out_specs=(placed,) * 4,
        check_vma=False,
    )
```

time: 679 us -> 18.9 us (0.03)
  the two profiles are of different devices: /device:TPU:8 before, /device:TPU:1 now
where the time goes in v1:
time: 18.9 us; the launch traced here: 18.7 us
  Pallas kernels  14.1 us (75%)
  local copies, waits for them, and re-layouts  3.86 us (20%)
  between operations  0.65 us (3%)
    pallas_call x1, Pallas kernels, local(): pl.pallas_call(functools.partial(kernel, nx, ny), out_shape=(out,) * 4, i...  14.1 us
    unnamed x10, local copies, waits for them, and re-layouts  3.86 us

profile of v1, /device:TPU:1, one launch (start us, length us, event | category | flops | bytes accessed | tf_op | source)
XLA Modules:
  0.0 18.7 jit_solution(5722927204897779470)
XLA Ops:
  0.6 14.1 %shard_map.46 = (f32[1,64,256]{2,1,0:T(8,128)}, f32[1,64,256]{2,1,0:T(8,128)}, f32[1,64,256]{2,1,0:T(8,128)}, f32[1,64,256]{2,1,0:T(8,128)}) custom-call(f32[1,64,256]{2,1,0:T(8,128)} %v_ref.1), custom_call_target="tpu_custom_call" | custom-call | tf_op jit(solution)/shard_map/pallas_call | solution.py:161
  14.8 0.0 copy-start.2
  14.8 1.5 %copy.9 = f32[1,64,256]{2,1,0:T(8,128)} copy(f32[1,64,256]{2,1,0:T(8,128)} %get-tuple-element.8) | data formatting | bytes 131072
  16.3 0.0 copy-done.2
  16.3 0.0 copy-start.1
  16.3 0.6 %copy.10 = f32[1,64,256]{2,1,0:T(8,128)} copy(f32[1,64,256]{2,1,0:T(8,128)S(1)} %copy-done.2) | data formatting | bytes 131072
  16.9 0.2 %copy-done.1 = f32[1,64,256]{2,1,0:T(8,128)S(1)} copy-done((f32[1,64,256]{2,1,0:T(8,128)S(1)}, f32[1,64,256]{2,1,0:T(8,128)}, u32[]{:S(2)}) %copy-start.1) | copy-done | bytes 65560
  17.2 0.0 copy-start
  17.2 0.6 %copy.11 = f32[1,64,256]{2,1,0:T(8,128)} copy(f32[1,64,256]{2,1,0:T(8,128)S(1)} %copy-done.1) | data formatting | bytes 131072
  17.8 0.2 %copy-done = f32[1,64,256]{2,1,0:T(8,128)S(1)} copy-done((f32[1,64,256]{2,1,0:T(8,128)S(1)}, f32[1,64,256]{2,1,0:T(8,128)}, u32[]{:S(2)}) %copy-start) | copy-done | bytes 65560
  18.0 0.6 %copy.12 = f32[1,64,256]{2,1,0:T(8,128)} copy(f32[1,64,256]{2,1,0:T(8,128)S(1)} %copy-done) | data formatting | bytes 131072
Async XLA Ops:
  14.8 1.5 %copy-start.2 = (f32[1,64,256]{2,1,0:T(8,128)S(1)}, f32[1,64,256]{2,1,0:T(8,128)}, u32[]{:S(2)}) copy-start(f32[1,64,256]{2,1,0:T(8,128)} %get-tuple-element.9) | copy-start | bytes 196612
  16.3 0.9 %copy-start.1 = (f32[1,64,256]{2,1,0:T(8,128)S(1)}, f32[1,64,256]{2,1,0:T(8,128)}, u32[]{:S(2)}) copy-start(f32[1,64,256]{2,1,0:T(8,128)} %get-tuple-element.10) | copy-start | bytes 196612
  17.2 0.9 %copy-start = (f32[1,64,256]{2,1,0:T(8,128)S(1)}, f32[1,64,256]{2,1,0:T(8,128)}, u32[]{:S(2)}) copy-start(f32[1,64,256]{2,1,0:T(8,128)} %get-tuple-element.11) | copy-start | bytes 196612

commit v2 on v1

v2 whole, which is shorter than its diff:
```python
import functools
import math

import jax
import jax.numpy as jnp
from jax import lax
from jax.experimental import pallas as pl
from jax.experimental.pallas import tpu as pltpu
from jax.sharding import PartitionSpec as P

FIRST_NEAR = 7.0 / 9.0
FIRST_FAR = 1.0 / 36.0
SECOND_NEAR = 12.0 / 11.0
SECOND_FAR = 3.0 / 44.0
COUPLINGS = (1.0 / 3.0, 2.0 / 11.0)
MESH = pl.DeviceIdType.MESH
HALO = 24
F32 = jnp.float32
BF16 = jnp.bfloat16


def green(coupling):
    root = math.sqrt(1.0 - 4.0 * coupling * coupling)
    return (1.0 - root) / (2.0 * coupling), 1.0 / root


def powers(coupling, distance):
    ratio, scale = green(coupling)
    size = scale * jnp.exp(distance.astype(F32) * math.log(ratio))
    return jnp.where(distance % 2 == 0, size, -size)


def stencils(u, axis):
    n = u.shape[axis]
    plus_one = pltpu.roll(u, n - 1, axis)
    minus_one = pltpu.roll(u, 1, axis)
    plus_two = pltpu.roll(u, n - 2, axis)
    minus_two = pltpu.roll(u, 2, axis)
    first = FIRST_NEAR * (plus_one - minus_one) + FIRST_FAR * (plus_two - minus_two)
    second = SECOND_NEAR * (plus_one - 2.0 * u + minus_one) + SECOND_FAR * (
        plus_two - 2.0 * u + minus_two
    )
    return first, second


def iota(shape, axis):
    return lax.broadcasted_iota(jnp.int32, shape, axis)


def split(a):
    high = a.astype(BF16)
    return high, (a - high.astype(F32)).astype(BF16)


def dot(a, b):
    return jnp.dot(a, b, preferred_element_type=F32)


def dot3(a, b):
    ah, al = split(a)
    bh, bl = split(b)
    return dot(ah, bh) + dot(al, bh) + dot(ah, bl)


def kernel(
    nx, ny, v_ref, dx_ref, dy_ref, dxx_ref, dyy_ref, u_ref, xl, xr, yl, yr, load_sem, send, recv, ready
):
    ix = lax.axis_index("gx")
    iy = lax.axis_index("gy")
    up = {"gx": lax.rem(ix + 1, nx)}
    down = {"gx": lax.rem(ix + nx - 1, nx)}
    right = {"gy": lax.rem(iy + 1, ny)}
    left = {"gy": lax.rem(iy + ny - 1, ny)}
    rows, cols = u_ref.shape
    first = ix == 0
    last = ix == nx - 1
    odd = lax.rem(iy, 2)

    def signal(semaphore, other):
        pl.semaphore_signal(semaphore, inc=1, device_id=other, device_id_type=MESH)

    def remote(k, src, dst, other):
        return pltpu.make_async_remote_copy(
            src_ref=src,
            dst_ref=dst,
            send_sem=send.at[k],
            recv_sem=recv.at[k],
            device_id=other,
            device_id_type=MESH,
        )

    barrier = pltpu.get_barrier_semaphore()
    signal(barrier, down)
    pl.when(jnp.logical_not(last))(lambda: signal(barrier, up))

    @pl.when(odd == 1)
    def _():
        signal(barrier, left)
        signal(barrier, right)

    load = pltpu.make_async_copy(v_ref.at[0], u_ref, load_sem)
    to_up = remote(0, v_ref.at[0, pl.ds(rows - HALO, HALO), :], xl, up)
    to_down = remote(1, v_ref.at[0, pl.ds(0, HALO), :], xr, down)
    to_right = remote(2, v_ref.at[0, :, pl.ds(cols - 128, 128)], yl, right)
    to_left = remote(3, v_ref.at[0, :, pl.ds(0, 128)], yr, left)

    pl.semaphore_wait(barrier, jnp.where(first, 1, 2) + 2 * (1 - odd))
    to_up.start()
    load.start()
    pl.when(last)(lambda: signal(ready.at[2], up))
    pl.when(jnp.logical_not(first))(lambda: to_down.start())

    @pl.when(odd == 0)
    def _():
        signal(ready.at[0], right)
        signal(ready.at[1], left)

    @pl.when(odd == 1)
    def _():
        pl.semaphore_wait(ready.at[0], 1)
        pl.semaphore_wait(ready.at[1], 1)

    to_right.start()
    to_left.start()

    load.wait()
    u = u_ref[...]
    row = iota((rows, cols), 0)
    col = iota((rows, cols), 1)
    inner = (row >= 2) & (row < rows - 2)
    rx = [jnp.where(inner, s, 0.0) for s in stencils(u, 0)]
    distance = jnp.abs(iota((rows, rows), 0) - iota((rows, rows), 1))
    for out, c, s in zip((dx_ref, dxx_ref), COUPLINGS, rx):
        out[0] = dot3(powers(c, distance), s)
    inner = (col >= 2) & (col < cols - 2)
    ry = [jnp.where(inner, s, 0.0) for s in stencils(u, 1)]
    distance = jnp.abs(iota((cols, cols), 0) - iota((cols, cols), 1))
    fy = [dot3(s, powers(c, distance)) for c, s in zip(COUPLINGS, ry)]

    edge = HALO + 8
    place = iota((edge, cols), 0)
    tail = iota((HALO, cols), 0)
    below = []
    above = []
    for c in COUPLINGS:
        _, scale = green(c)
        below.append(
            (
                jnp.where((place >= 2) & (place <= HALO), powers(c, jnp.abs(HALO - place)), 0.0) / scale,
                powers(c, tail),
                powers(c, jnp.abs(tail - 1)),
            )
        )
        above.append(
            (
                jnp.where((place >= 7) & (place < edge - 2), powers(c, jnp.abs(place - 7)), 0.0) / scale,
                powers(c, HALO - 1 - tail),
                powers(c, jnp.abs(HALO - 2 - tail)),
            )
        )
    lane = iota((rows, 128), 1)
    source = iota((128, 128), 0)
    target = iota((128, 128), 1)
    sides = [
        [split(powers(c, jnp.abs(target - source + shift))) for c in COUPLINGS] for shift in (64, -64)
    ]
    near = [pltpu.roll(u[:, :128], 64, 1), pltpu.roll(u[:, cols - 128 :], 64, 1)]

    def multiply(a, b):
        ah, al = split(a)
        return dot(ah, b[0]) + dot(al, b[0]) + dot(ah, b[1])

    to_right.wait_recv()
    to_left.wait_recv()
    lower = stencils(jnp.where(lane < 64, pltpu.roll(yl[...], 64, 1), near[0]), 1)
    upper = stencils(jnp.where(lane < 64, near[1], pltpu.roll(yr[...], 64, 1)), 1)
    for k, out in enumerate((dy_ref, dyy_ref)):
        low = jnp.where((lane >= 2) & (lane < 66), lower[k], 0.0)
        high = jnp.where((lane >= 62) & (lane < 126), upper[k], 0.0)
        out[0] = fy[k] + jnp.concatenate(
            [multiply(low, sides[0][k]), multiply(high, sides[1][k])], axis=1
        )

    @pl.when(first)
    def _():
        pl.semaphore_wait(ready.at[2], 1)
        to_down.start()

    to_down.wait_recv()
    upper = stencils(jnp.concatenate([u[rows - 8 :], xr[...]], axis=0), 0)
    for k, out in enumerate((dx_ref, dxx_ref)):
        weight, far, close = above[k]
        total = jnp.sum(weight * upper[k], axis=0, keepdims=True)
        out[0, pl.ds(rows - HALO, HALO), :] += far * total + close * upper[k][6:7]

    to_up.wait_recv()
    lower = stencils(jnp.concatenate([xl[...], u[:8]], axis=0), 0)
    for k, out in enumerate((dx_ref, dxx_ref)):
        weight, far, close = below[k]
        total = jnp.sum(weight * lower[k], axis=0, keepdims=True)
        out[0, pl.ds(0, HALO), :] += far * total + close * lower[k][HALO + 1 : HALO + 2]

    for copy in (to_up, to_down, to_right, to_left):
        copy.wait_send()


def writer(*refs):
    sources, targets, sem = refs[:4], refs[4:8], refs[8]
    copies = [pltpu.make_async_copy(s, t, sem.at[k]) for k, (s, t) in enumerate(zip(sources, targets))]
    for copy in copies:
        copy.start()
    for copy in copies:
        copy.wait()


def local(nx, ny, velocity):
    _, rows, cols = velocity.shape
    out = jax.ShapeDtypeStruct(velocity.shape, F32)
    fields = pl.pallas_call(
        functools.partial(kernel, nx, ny),
        out_shape=(pltpu.VMEM(velocity.shape, F32),) * 4,
        in_specs=[pl.BlockSpec(memory_space=pl.ANY)],
        out_specs=[pl.BlockSpec(memory_space=pltpu.VMEM)] * 4,
        scratch_shapes=[
            pltpu.VMEM((rows, cols), F32),
            pltpu.VMEM((HALO, cols), F32),
            pltpu.VMEM((HALO, cols), F32),
            pltpu.VMEM((rows, 128), F32),
            pltpu.VMEM((rows, 128), F32),
            pltpu.SemaphoreType.DMA,
            pltpu.SemaphoreType.DMA((4,)),
            pltpu.SemaphoreType.DMA((4,)),
            pltpu.SemaphoreType.REGULAR((3,)),
        ],
        compiler_params=pltpu.CompilerParams(collective_id=0, has_side_effects=True),
    )(velocity)
    return pl.pallas_call(
        writer,
        out_shape=(out,) * 4,
        in_specs=[pl.BlockSpec(memory_space=pltpu.VMEM)] * 4,
        out_specs=[pl.BlockSpec(memory_space=pl.ANY)] * 4,
        scratch_shapes=[pltpu.SemaphoreType.DMA((4,))],
    )(*[pltpu.with_memory_space_constraint(f, pltpu.VMEM) for f in fields])


def solution(mesh):
    placed = P(None, "gx", "gy")
    return jax.shard_map(
        functools.partial(local, mesh.shape["gx"], mesh.shape["gy"]),
        mesh=mesh,
        in_specs=(placed,),
        out_specs=(placed,) * 4,
        check_vma=False,
    )
```

time: 18.9 us -> 12.7 us (0.67)
  the two profiles are of different devices: /device:TPU:1 before, /device:TPU:8 now
where the time goes in v2:
time: 12.7 us; the launch traced here: 12.6 us
  Pallas kernels  11.9 us (94%)
  between operations  0.64 us (5%)
    pallas_call x1, Pallas kernels, local(): pl.pallas_call(functools.partial(kernel, nx, ny), out_shape=(pltpu.VMEM(v...  11.2 us
    pallas_call x1, Pallas kernels, local(): pl.pallas_call(writer, out_shape=(out,) * 4, in_specs=[pl.BlockSpec(memor...  0.73 us

profile of v2, /device:TPU:8, one launch (start us, length us, event | category | flops | bytes accessed | tf_op | source)
XLA Modules:
  0.0 12.6 jit_solution(17003528121813708623)
XLA Ops:
  0.6 11.2 %shard_map.46 = (f32[1,64,256]{2,1,0:T(8,128)S(1)}, f32[1,64,256]{2,1,0:T(8,128)S(1)}, f32[1,64,256]{2,1,0:T(8,128)S(1)}, f32[1,64,256]{2,1,0:T(8,128)S(1)}) custom-call(f32[1,64,256]{2,1,0:T(8,128)} %v_ref.1), custom_call_target="tpu_custom_call" | custom-call | tf_op jit(solution)/shard_map/pallas_call | solution.py:219
  11.9 0.7 %shard_map.47 = (f32[1,64,256]{2,1,0:T(8,128)}, f32[1,64,256]{2,1,0:T(8,128)}, f32[1,64,256]{2,1,0:T(8,128)}, f32[1,64,256]{2,1,0:T(8,128)}) custom-call(f32[1,64,256]{2,1,0:T(8,128)S(1)} %get-tuple-element.8.refs_0_, f32[1,64,256]{2,1,0:T(8,128)S(1)} %get-tuple-element.9.refs_1_, f32[1,64,256]{2,1,0:T(8,128)S(1)} %get-tuple-element.10.refs_2_, ...), custom_call_target="tpu_custom_call" | custom-call | tf_op jit(solution)/shard_map/pallas_call | solution.py:237

commit v3 on v2

--- a/solution.py
+++ b/solution.py
@@ -74,6 +74,7 @@
     rows, cols = u_ref.shape
     first = ix == 0
     last = ix == nx - 1
+    before = ix == nx - 2
     odd = lax.rem(iy, 2)
 
     def signal(semaphore, other):
@@ -91,9 +92,9 @@
 
     barrier = pltpu.get_barrier_semaphore()
     signal(barrier, down)
-    pl.when(jnp.logical_not(last))(lambda: signal(barrier, up))
-
-    @pl.when(odd == 1)
+    pl.when(ix < nx - 2)(lambda: signal(barrier, up))
+
+    @pl.when((odd == 1) & (ix < nx - 1))
     def _():
         signal(barrier, left)
         signal(barrier, right)
@@ -104,24 +105,37 @@
     to_right = remote(2, v_ref.at[0, :, pl.ds(cols - 128, 128)], yl, right)
     to_left = remote(3, v_ref.at[0, :, pl.ds(0, 128)], yr, left)
 
-    pl.semaphore_wait(barrier, jnp.where(first, 1, 2) + 2 * (1 - odd))
+    def answer_sides():
+        signal(ready.at[0], right)
+        signal(ready.at[1], left)
+
+    def await_sides():
+        pl.semaphore_wait(ready.at[0], 1)
+        pl.semaphore_wait(ready.at[1], 1)
+
+    along_x = jnp.where(first | last, 1, 2)
+    along_y = jnp.where(last, 0, 2 * (1 - odd))
+    pl.semaphore_wait(barrier, along_x + along_y)
     to_up.start()
     load.start()
     pl.when(last)(lambda: signal(ready.at[2], up))
-    pl.when(jnp.logical_not(first))(lambda: to_down.start())
-
-    @pl.when(odd == 0)
-    def _():
-        signal(ready.at[0], right)
-        signal(ready.at[1], left)
-
-    @pl.when(odd == 1)
-    def _():
-        pl.semaphore_wait(ready.at[0], 1)
-        pl.semaphore_wait(ready.at[1], 1)
-
-    to_right.start()
-    to_left.start()
+
+    @pl.when(jnp.logical_not(last))
+    def _():
+        pl.when(jnp.logical_not(first))(lambda: to_down.start())
+        pl.when(odd == 0)(answer_sides)
+
+        @pl.when(odd == 1)
+        def _():
+            await_sides()
+
+            @pl.when(before)
+            def _():
+                answer_sides()
+                signal(ready.at[3], up)
+
+        to_right.start()
+        to_left.start()
 
     load.wait()
     u = u_ref[...]
@@ -169,6 +183,18 @@
     def multiply(a, b):
         ah, al = split(a)
         return dot(ah, b[0]) + dot(al, b[0]) + dot(ah, b[1])
+
+    @pl.when(before & (odd == 0))
+    def _():
+        await_sides()
+        signal(ready.at[3], up)
+
+    @pl.when(last)
+    def _():
+        pl.semaphore_wait(ready.at[3], 1)
+        to_right.start()
+        to_left.start()
+        to_down.start()
 
     to_right.wait_recv()
     to_left.wait_recv()
@@ -230,7 +256,7 @@
             pltpu.SemaphoreType.DMA,
             pltpu.SemaphoreType.DMA((4,)),
             pltpu.SemaphoreType.DMA((4,)),
-            pltpu.SemaphoreType.REGULAR((3,)),
+            pltpu.SemaphoreType.REGULAR((4,)),
         ],
         compiler_params=pltpu.CompilerParams(collective_id=0, has_side_effects=True),
     )(velocity)

time: 12.7 us -> 11.9 us (0.937)
  Pallas kernels: 11.9 us -> 11.1 us
    pallas_call x1, Pallas kernels: 11.2 us -> 10.4 us  [local(): pl.pallas_call(functools.partial(kernel, nx, ny), out_shape=(pltpu.VMEM(v...]
where the time goes in v3:
time: 11.9 us; the launch traced here: 11.8 us
  Pallas kernels  11.1 us (93%)
  between operations  0.64 us (5%)
    pallas_call x1, Pallas kernels, local(): pl.pallas_call(functools.partial(kernel, nx, ny), out_shape=(pltpu.VMEM(v...  10.4 us
    pallas_call x1, Pallas kernels, local(): pl.pallas_call(writer, out_shape=(out,) * 4, in_specs=[pl.BlockSpec(memor...  0.73 us

profile of v3, /device:TPU:8, one launch (start us, length us, event | category | flops | bytes accessed | tf_op | source)
XLA Modules:
  0.0 11.8 jit_solution(17772847871675253941)
XLA Ops:
  0.6 10.4 %shard_map.46 = (f32[1,64,256]{2,1,0:T(8,128)S(1)}, f32[1,64,256]{2,1,0:T(8,128)S(1)}, f32[1,64,256]{2,1,0:T(8,128)S(1)}, f32[1,64,256]{2,1,0:T(8,128)S(1)}) custom-call(f32[1,64,256]{2,1,0:T(8,128)} %v_ref.1), custom_call_target="tpu_custom_call" | custom-call | tf_op jit(solution)/shard_map/pallas_call | solution.py:245
  11.0 0.7 %shard_map.47 = (f32[1,64,256]{2,1,0:T(8,128)}, f32[1,64,256]{2,1,0:T(8,128)}, f32[1,64,256]{2,1,0:T(8,128)}, f32[1,64,256]{2,1,0:T(8,128)}) custom-call(f32[1,64,256]{2,1,0:T(8,128)S(1)} %get-tuple-element.8.refs_0_, f32[1,64,256]{2,1,0:T(8,128)S(1)} %get-tuple-element.9.refs_1_, f32[1,64,256]{2,1,0:T(8,128)S(1)} %get-tuple-element.10.refs_2_, ...), custom_call_target="tpu_custom_call" | custom-call | tf_op jit(solution)/shard_map/pallas_call | solution.py:263

commit v4 on v3

v4 whole, which is shorter than its diff:
```python
import functools
import math

import jax
import jax.numpy as jnp
from jax import lax
from jax.experimental import pallas as pl
from jax.experimental.pallas import tpu as pltpu
from jax.sharding import PartitionSpec as P

FIRST_NEAR = 7.0 / 9.0
FIRST_FAR = 1.0 / 36.0
SECOND_NEAR = 12.0 / 11.0
SECOND_FAR = 3.0 / 44.0
COUPLINGS = (1.0 / 3.0, 2.0 / 11.0)
MESH = pl.DeviceIdType.MESH
HALO = 24
F32 = jnp.float32
BF16 = jnp.bfloat16


def green(coupling):
    root = math.sqrt(1.0 - 4.0 * coupling * coupling)
    return (1.0 - root) / (2.0 * coupling), 1.0 / root


def powers(coupling, distance):
    ratio, scale = green(coupling)
    size = scale * jnp.exp(distance.astype(F32) * math.log(ratio))
    return jnp.where(distance % 2 == 0, size, -size)


def stencils(u, axis):
    n = u.shape[axis]
    plus_one = pltpu.roll(u, n - 1, axis)
    minus_one = pltpu.roll(u, 1, axis)
    plus_two = pltpu.roll(u, n - 2, axis)
    minus_two = pltpu.roll(u, 2, axis)
    first = FIRST_NEAR * (plus_one - minus_one) + FIRST_FAR * (plus_two - minus_two)
    second = SECOND_NEAR * (plus_one - 2.0 * u + minus_one) + SECOND_FAR * (
        plus_two - 2.0 * u + minus_two
    )
    return first, second


def iota(shape, axis):
    return lax.broadcasted_iota(jnp.int32, shape, axis)


def split(a):
    high = a.astype(BF16)
    return high, (a - high.astype(F32)).astype(BF16)


def dot(a, b):
    return jnp.dot(a, b, preferred_element_type=F32)


def kernel(
    nx,
    ny,
    v_ref,
    dx_ref,
    dy_ref,
    dxx_ref,
    dyy_ref,
    edge_ref,
    weight_ref,
    u_ref,
    xr,
    yl,
    yr,
    load_sem,
    send,
    recv,
    ready,
):
    ix = lax.axis_index("gx")
    iy = lax.axis_index("gy")
    up = {"gx": jnp.where(ix == nx - 1, 0, ix + 1)}
    down = {"gx": jnp.where(ix == 0, nx - 1, ix - 1)}
    right = {"gy": jnp.where(iy == ny - 1, 0, iy + 1)}
    left = {"gy": jnp.where(iy == 0, ny - 1, iy - 1)}
    rows, cols = u_ref.shape
    first = ix == 0
    last = ix == nx - 1
    before = ix == nx - 2
    odd = lax.rem(iy, 2)

    def signal(semaphore, other):
        pl.semaphore_signal(semaphore, inc=1, device_id=other, device_id_type=MESH)

    def remote(k, src, dst, other):
        return pltpu.make_async_remote_copy(
            src_ref=src,
            dst_ref=dst,
            send_sem=send.at[k],
            recv_sem=recv.at[k],
            device_id=other,
            device_id_type=MESH,
        )

    load = pltpu.make_async_copy(v_ref.at[0], u_ref, load_sem)
    to_up = remote(0, v_ref.at[0, pl.ds(rows - HALO, HALO), :], edge_ref.at[pl.ds(0, HALO), :], up)
    to_down = remote(1, v_ref.at[0, pl.ds(0, HALO), :], xr, down)
    to_right = remote(2, v_ref.at[0, :, pl.ds(cols - 128, 128)], yl, right)
    to_left = remote(3, v_ref.at[0, :, pl.ds(0, 128)], yr, left)

    barrier = pltpu.get_barrier_semaphore()
    signal(barrier, down)

    @pl.when(last)
    def _():
        pl.semaphore_wait(barrier, 1)
        to_up.start()
        signal(ready.at[2], up)

    def greet_sides():
        signal(barrier, left)
        signal(barrier, right)

    def answer_sides():
        signal(ready.at[0], right)
        signal(ready.at[1], left)

    @pl.when(jnp.logical_not(last))
    def _():
        pl.when(jnp.logical_not(before))(lambda: signal(barrier, up))
        pl.when((odd == 1) & jnp.logical_not(before))(greet_sides)
        pl.semaphore_wait(barrier, jnp.where(first, 1, 2) + 2 * (1 - odd))
        to_up.start()

        @pl.when(before)
        def _():
            signal(ready.at[3], up)
            pl.when(odd == 0)(lambda: signal(ready.at[4], up))
            pl.when(odd == 1)(greet_sides)

        pl.when(jnp.logical_not(first))(lambda: to_down.start())
        pl.when(odd == 0)(answer_sides)

        @pl.when(odd == 1)
        def _():
            pl.semaphore_wait(ready.at[0], 1)
            pl.semaphore_wait(ready.at[1], 1)
            pl.when(before)(lambda: signal(ready.at[4], up))

        to_right.start()
        to_left.start()

    load.start()
    distance = jnp.abs(iota((rows, rows), 0) - iota((rows, rows), 1))
    across = [split(powers(c, distance)) for c in COUPLINGS]
    distance = jnp.abs(iota((cols, cols), 0) - iota((cols, cols), 1))
    along = [split(powers(c, distance)) for c in COUPLINGS]
    edge = HALO + 8
    place = iota((edge, cols), 0)
    tail = iota((HALO, cols), 0)
    above = []
    for k, c in enumerate(COUPLINGS):
        _, scale = green(c)
        weight_ref[k, pl.ds(0, edge), :] = (
            jnp.where((place >= 2) & (place <= HALO), powers(c, jnp.abs(HALO - place)), 0.0) / scale
        )
        weight_ref[k, pl.ds(edge, HALO), :] = powers(c, tail)
        weight_ref[k, pl.ds(edge + HALO, HALO), :] = powers(c, jnp.abs(tail - 1))
        above.append(
            (
                jnp.where((place >= 7) & (place < edge - 2), powers(c, jnp.abs(place - 7)), 0.0) / scale,
                powers(c, HALO - 1 - tail),
                powers(c, jnp.abs(HALO - 2 - tail)),
            )
        )
    lane = iota((rows, 128), 1)
    source = iota((128, 128), 0)
    target = iota((128, 128), 1)
    sides = [
        [split(powers(c, jnp.abs(target - source + shift))) for c in COUPLINGS] for shift in (64, -64)
    ]
    def multiply(a, b):
        ah, al = split(a)
        return dot(ah, b[0]) + dot(al, b[0]) + dot(ah, b[1])

    load.wait()
    u = u_ref[...]
    edge_ref[pl.ds(HALO, 8), :] = u[:8]
    near = [pltpu.roll(u[:, :128], 64, 1), pltpu.roll(u[:, cols - 128 :], 64, 1)]

    row = iota((rows, cols), 0)
    col = iota((rows, cols), 1)
    inner = (row >= 2) & (row < rows - 2)
    for out, g, s in zip((dx_ref, dxx_ref), across, stencils(u, 0)):
        high, low = split(jnp.where(inner, s, 0.0))
        out[0] = dot(g[0], high) + dot(g[1], high) + dot(g[0], low)
    inner = (col >= 2) & (col < cols - 2)
    fy = [multiply(jnp.where(inner, s, 0.0), g) for g, s in zip(along, stencils(u, 1))]

    @pl.when(last)
    def _():
        pl.semaphore_wait(ready.at[3], 1)
        to_down.start()
        pl.semaphore_wait(ready.at[4], 1)
        to_right.start()
        to_left.start()

    to_right.wait_recv()
    to_left.wait_recv()
    lower = stencils(jnp.where(lane < 64, pltpu.roll(yl[...], 64, 1), near[0]), 1)
    upper = stencils(jnp.where(lane < 64, near[1], pltpu.roll(yr[...], 64, 1)), 1)
    for k, out in enumerate((dy_ref, dyy_ref)):
        low = jnp.where((lane >= 2) & (lane < 66), lower[k], 0.0)
        high = jnp.where((lane >= 62) & (lane < 126), upper[k], 0.0)
        out[0] = fy[k] + jnp.concatenate(
            [multiply(low, sides[0][k]), multiply(high, sides[1][k])], axis=1
        )

    @pl.when(first)
    def _():
        pl.semaphore_wait(ready.at[2], 1)
        remote(1, u_ref.at[pl.ds(0, HALO), :], xr, down).start()

    to_down.wait_recv()
    upper = stencils(jnp.concatenate([u[rows - 8 :], xr[...]], axis=0), 0)
    for k, out in enumerate((dx_ref, dxx_ref)):
        weight, far, close = above[k]
        total = jnp.sum(weight * upper[k], axis=0, keepdims=True)
        out[0, pl.ds(rows - HALO, HALO), :] += far * total + close * upper[k][6:7]

    to_up.wait_recv()
    for copy in (to_up, to_down, to_right, to_left):
        copy.wait_send()


def finish(
    dx_in, dy_in, dxx_in, dyy_in, edge_ref, weight_ref, dx_ref, dy_ref, dxx_ref, dyy_ref, low, sem
):
    rest = pl.ds(HALO, dx_in.shape[1] - HALO)
    copies = [
        pltpu.make_async_copy(dy_in, dy_ref, sem.at[0]),
        pltpu.make_async_copy(dyy_in, dyy_ref, sem.at[1]),
        pltpu.make_async_copy(dx_in.at[0, rest, :], dx_ref.at[0, rest, :], sem.at[2]),
        pltpu.make_async_copy(dxx_in.at[0, rest, :], dxx_ref.at[0, rest, :], sem.at[3]),
    ]
    for copy in copies:
        copy.start()
    edge = HALO + 8
    head = pl.ds(0, HALO)
    lower = stencils(edge_ref[...], 0)
    for k, (part, out) in enumerate(((dx_in, dx_ref), (dxx_in, dxx_ref))):
        total = jnp.sum(weight_ref[k, pl.ds(0, edge), :] * lower[k], axis=0, keepdims=True)
        low[k] = (
            part[0, head, :]
            + weight_ref[k, pl.ds(edge, HALO), :] * total
            + weight_ref[k, pl.ds(edge + HALO, HALO), :] * lower[k][HALO + 1 : HALO + 2]
        )
        copy = pltpu.make_async_copy(low.at[k], out.at[0, head, :], sem.at[4 + k])
        copy.start()
        copies.append(copy)
    for copy in copies:
        copy.wait()


def local(nx, ny, velocity):
    _, rows, cols = velocity.shape
    out = jax.ShapeDtypeStruct(velocity.shape, F32)
    vmem = pl.BlockSpec(memory_space=pltpu.VMEM)
    anywhere = pl.BlockSpec(memory_space=pl.ANY)
    fields = pl.pallas_call(
        functools.partial(kernel, nx, ny),
        out_shape=(pltpu.VMEM(velocity.shape, F32),) * 4
        + (pltpu.VMEM((HALO + 8, cols), F32), pltpu.VMEM((2, 3 * HALO + 8, cols), F32)),
        in_specs=[anywhere],
        out_specs=[vmem] * 6,
        scratch_shapes=[
            pltpu.VMEM((rows, cols), F32),
            pltpu.VMEM((HALO, cols), F32),
            pltpu.VMEM((rows, 128), F32),
            pltpu.VMEM((rows, 128), F32),
            pltpu.SemaphoreType.DMA,
            pltpu.SemaphoreType.DMA((4,)),
            pltpu.SemaphoreType.DMA((4,)),
            pltpu.SemaphoreType.REGULAR((5,)),
        ],
        compiler_params=pltpu.CompilerParams(collective_id=0, has_side_effects=True),
    )(velocity)
    return pl.pallas_call(
        finish,
        out_shape=(out,) * 4,
        in_specs=[vmem] * 6,
        out_specs=[anywhere] * 4,
        scratch_shapes=[pltpu.VMEM((2, HALO, cols), F32), pltpu.SemaphoreType.DMA((6,))],
    )(*[pltpu.with_memory_space_constraint(f, pltpu.VMEM) for f in fields])


def solution(mesh):
    placed = P(None, "gx", "gy")
    return jax.shard_map(
        functools.partial(local, mesh.shape["gx"], mesh.shape["gy"]),
        mesh=mesh,
        in_specs=(placed,),
        out_specs=(placed,) * 4,
        check_vma=False,
    )
```

time: 11.9 us -> 11.9 us (level)
  no operation moved by 1% of the time
where the time goes in v4:
time: 11.9 us; the launch traced here: 11.7 us
  Pallas kernels  11.1 us (93%)
  between operations  0.64 us (5%)
    pallas_call x1, Pallas kernels, local(): pl.pallas_call(functools.partial(kernel, nx, ny), out_shape=(pltpu.VMEM(v...  10.4 us
    pallas_call x1, Pallas kernels, local(): pl.pallas_call(finish, out_shape=(out,) * 4, in_specs=[vmem] * 6, out_spe...  0.74 us

profile of v4, /device:TPU:8, one launch (start us, length us, event | category | flops | bytes accessed | tf_op | source)
XLA Modules:
  0.0 11.7 jit_solution(6528733384103736284)
XLA Ops:
  0.6 10.4 %shard_map.46 = (f32[1,64,256]{2,1,0:T(8,128)S(1)}, f32[1,64,256]{2,1,0:T(8,128)S(1)}, f32[1,64,256]{2,1,0:T(8,128)S(1)}, f32[1,64,256]{2,1,0:T(8,128)S(1)}, f32...) custom-call(f32[1,64,256]{2,1,0:T(8,128)} %v_ref.1), custom_call_target="tpu_custom_call" | custom-call | tf_op jit(solution)/shard_map/pallas_call | solution.py:268
  11.0 0.7 %shard_map.47 = (f32[1,64,256]{2,1,0:T(8,128)}, f32[1,64,256]{2,1,0:T(8,128)}, f32[1,64,256]{2,1,0:T(8,128)}, f32[1,64,256]{2,1,0:T(8,128)}) custom-call(f32[1,64,256]{2,1,0:T(8,128)S(1)} %get-tuple-element.10.dx_in, f32[1,64,256]{2,1,0:T(8,128)S(1)} %get-tuple-element.11.dy_in, f32[1,64,256]{2,1,0:T(8,128)S(1)} %get-tuple-element.12.dxx_in, ...), custom_call_target="tpu_custom_call" | custom-call | tf_op jit(solution)/shard_map/pallas_call | solution.py:286

commit v5 on v4

--- a/solution.py
+++ b/solution.py
@@ -70,6 +70,7 @@
     xr,
     yl,
     yr,
+    pool,
     load_sem,
     send,
     recv,
@@ -94,17 +95,21 @@
         return pltpu.make_async_remote_copy(
             src_ref=src,
             dst_ref=dst,
-            send_sem=send.at[k],
+            send_sem=send,
             recv_sem=recv.at[k],
             device_id=other,
             device_id_type=MESH,
         )
 
+    def take(count, semaphore):
+        part = pool.at[pl.ds(0, count), :]
+        pltpu.make_async_copy(part, part, semaphore).wait()
+
     load = pltpu.make_async_copy(v_ref.at[0], u_ref, load_sem)
     to_up = remote(0, v_ref.at[0, pl.ds(rows - HALO, HALO), :], edge_ref.at[pl.ds(0, HALO), :], up)
     to_down = remote(1, v_ref.at[0, pl.ds(0, HALO), :], xr, down)
-    to_right = remote(2, v_ref.at[0, :, pl.ds(cols - 128, 128)], yl, right)
-    to_left = remote(3, v_ref.at[0, :, pl.ds(0, 128)], yr, left)
+    to_right = remote(1, v_ref.at[0, :, pl.ds(cols - 128, 128)], yl, right)
+    to_left = remote(1, v_ref.at[0, :, pl.ds(0, 128)], yr, left)
 
     barrier = pltpu.get_barrier_semaphore()
     signal(barrier, down)
@@ -113,7 +118,7 @@
     def _():
         pl.semaphore_wait(barrier, 1)
         to_up.start()
-        signal(ready.at[2], up)
+        signal(ready.at[1], up)
 
     def greet_sides():
         signal(barrier, left)
@@ -121,7 +126,7 @@
 
     def answer_sides():
         signal(ready.at[0], right)
-        signal(ready.at[1], left)
+        signal(ready.at[0], left)
 
     @pl.when(jnp.logical_not(last))
     def _():
@@ -132,8 +137,8 @@
 
         @pl.when(before)
         def _():
-            signal(ready.at[3], up)
-            pl.when(odd == 0)(lambda: signal(ready.at[4], up))
+            signal(ready.at[0], up)
+            pl.when(odd == 0)(lambda: signal(ready.at[1], up))
             pl.when(odd == 1)(greet_sides)
 
         pl.when(jnp.logical_not(first))(lambda: to_down.start())
@@ -141,9 +146,8 @@
 
         @pl.when(odd == 1)
         def _():
-            pl.semaphore_wait(ready.at[0], 1)
-            pl.semaphore_wait(ready.at[1], 1)
-            pl.when(before)(lambda: signal(ready.at[4], up))
+            pl.semaphore_wait(ready.at[0], 2)
+            pl.when(before)(lambda: signal(ready.at[1], up))
 
         to_right.start()
         to_left.start()
@@ -177,6 +181,7 @@
     sides = [
         [split(powers(c, jnp.abs(target - source + shift))) for c in COUPLINGS] for shift in (64, -64)
     ]
+
     def multiply(a, b):
         ah, al = split(a)
         return dot(ah, b[0]) + dot(al, b[0]) + dot(ah, b[1])
@@ -197,14 +202,18 @@
 
     @pl.when(last)
     def _():
-        pl.semaphore_wait(ready.at[3], 1)
+        pl.semaphore_wait(ready.at[0], 1)
         to_down.start()
-        pl.semaphore_wait(ready.at[4], 1)
+        pl.semaphore_wait(ready.at[1], 1)
         to_right.start()
         to_left.start()
 
-    to_right.wait_recv()
-    to_left.wait_recv()
+    @pl.when(first)
+    def _():
+        pl.semaphore_wait(ready.at[1], 1)
+        remote(1, u_ref.at[pl.ds(0, HALO), :], xr, down).start()
+
+    take(rows + HALO, recv.at[1])
     lower = stencils(jnp.where(lane < 64, pltpu.roll(yl[...], 64, 1), near[0]), 1)
     upper = stencils(jnp.where(lane < 64, near[1], pltpu.roll(yr[...], 64, 1)), 1)
     for k, out in enumerate((dy_ref, dyy_ref)):
@@ -214,12 +223,6 @@
             [multiply(low, sides[0][k]), multiply(high, sides[1][k])], axis=1
         )
 
-    @pl.when(first)
-    def _():
-        pl.semaphore_wait(ready.at[2], 1)
-        remote(1, u_ref.at[pl.ds(0, HALO), :], xr, down).start()
-
-    to_down.wait_recv()
     upper = stencils(jnp.concatenate([u[rows - 8 :], xr[...]], axis=0), 0)
     for k, out in enumerate((dx_ref, dxx_ref)):
         weight, far, close = above[k]
@@ -227,19 +230,18 @@
         out[0, pl.ds(rows - HALO, HALO), :] += far * total + close * upper[k][6:7]
 
     to_up.wait_recv()
-    for copy in (to_up, to_down, to_right, to_left):
-        copy.wait_send()
+    take(rows + 2 * HALO, send)
 
 
 def finish(
-    dx_in, dy_in, dxx_in, dyy_in, edge_ref, weight_ref, dx_ref, dy_ref, dxx_ref, dyy_ref, low, sem
+    dx_in, dy_in, dxx_in, dyy_in, edge_ref, weight_ref, dx_ref, dy_ref, dxx_ref, dyy_ref, low, pool, sem
 ):
     rest = pl.ds(HALO, dx_in.shape[1] - HALO)
     copies = [
-        pltpu.make_async_copy(dy_in, dy_ref, sem.at[0]),
-        pltpu.make_async_copy(dyy_in, dyy_ref, sem.at[1]),
-        pltpu.make_async_copy(dx_in.at[0, rest, :], dx_ref.at[0, rest, :], sem.at[2]),
-        pltpu.make_async_copy(dxx_in.at[0, rest, :], dxx_ref.at[0, rest, :], sem.at[3]),
+        pltpu.make_async_copy(dy_in, dy_ref, sem),
+        pltpu.make_async_copy(dyy_in, dyy_ref, sem),
+        pltpu.make_async_copy(dx_in.at[0, rest, :], dx_ref.at[0, rest, :], sem),
+        pltpu.make_async_copy(dxx_in.at[0, rest, :], dxx_ref.at[0, rest, :], sem),
     ]
     for copy in copies:
         copy.start()
@@ -253,11 +255,8 @@
             + weight_ref[k, pl.ds(edge, HALO), :] * total
             + weight_ref[k, pl.ds(edge + HALO, HALO), :] * lower[k][HALO + 1 : HALO + 2]
         )
-        copy = pltpu.make_async_copy(low.at[k], out.at[0, head, :], sem.at[4 + k])
-        copy.start()
-        copies.append(copy)
-    for copy in copies:
-        copy.wait()
+        pltpu.make_async_copy(low.at[k], out.at[0, head, :], sem).start()
+    pltpu.make_async_copy(pool, pool, sem).wait()
 
 
 def local(nx, ny, velocity):
@@ -276,10 +275,11 @@
             pltpu.VMEM((HALO, cols), F32),
             pltpu.VMEM((rows, 128), F32),
             pltpu.VMEM((rows, 128), F32),
+            pltpu.VMEM((rows + 2 * HALO, cols), F32),
             pltpu.SemaphoreType.DMA,
-            pltpu.SemaphoreType.DMA((4,)),
-            pltpu.SemaphoreType.DMA((4,)),
-            pltpu.SemaphoreType.REGULAR((5,)),
+            pltpu.SemaphoreType.DMA,
+            pltpu.SemaphoreType.DMA((2,)),
+            pltpu.SemaphoreType.REGULAR((2,)),
         ],
         compiler_params=pltpu.CompilerParams(collective_id=0, has_side_effects=True),
     )(velocity)
@@ -288,7 +288,11 @@
         out_shape=(out,) * 4,
         in_specs=[vmem] * 6,
         out_specs=[anywhere] * 4,
-        scratch_shapes=[pltpu.VMEM((2, HALO, cols), F32), pltpu.SemaphoreType.DMA((6,))],
+        scratch_shapes=[
+            pltpu.VMEM((2, HALO, cols), F32),
+            pltpu.VMEM((4 * rows, cols), F32),
+            pltpu.SemaphoreType.DMA,
+        ],
     )(*[pltpu.with_memory_space_constraint(f, pltpu.VMEM) for f in fields])
 
 

time: 11.9 us -> 11.7 us (0.983)
  no operation moved by 1% of the time
where the time goes in v5:
time: 11.7 us; the launch traced here: 11.6 us
  Pallas kernels  11 us (94%)
  between operations  0.64 us (5%)
    pallas_call x1, Pallas kernels, local(): pl.pallas_call(functools.partial(kernel, nx, ny), out_shape=(pltpu.VMEM(v...  10.3 us
    pallas_call x1, Pallas kernels, local(): pl.pallas_call(finish, out_shape=(out,) * 4, in_specs=[vmem] * 6, out_spe...  0.7 us

profile of v5, /device:TPU:8, one launch (start us, length us, event | category | flops | bytes accessed | tf_op | source)
XLA Modules:
  0.0 11.6 jit_solution(313389434169464019)
XLA Ops:
  0.6 10.3 %shard_map.46 = (f32[1,64,256]{2,1,0:T(8,128)S(1)}, f32[1,64,256]{2,1,0:T(8,128)S(1)}, f32[1,64,256]{2,1,0:T(8,128)S(1)}, f32[1,64,256]{2,1,0:T(8,128)S(1)}, f32...) custom-call(f32[1,64,256]{2,1,0:T(8,128)} %v_ref.1), custom_call_target="tpu_custom_call" | custom-call | tf_op jit(solution)/shard_map/pallas_call | solution.py:267
  10.9 0.7 %shard_map.47 = (f32[1,64,256]{2,1,0:T(8,128)}, f32[1,64,256]{2,1,0:T(8,128)}, f32[1,64,256]{2,1,0:T(8,128)}, f32[1,64,256]{2,1,0:T(8,128)}) custom-call(f32[1,64,256]{2,1,0:T(8,128)S(1)} %get-tuple-element.10.dx_in, f32[1,64,256]{2,1,0:T(8,128)S(1)} %get-tuple-element.11.dy_in, f32[1,64,256]{2,1,0:T(8,128)S(1)} %get-tuple-element.12.dxx_in, ...), custom_call_target="tpu_custom_call" | custom-call | tf_op jit(solution)/shard_map/pallas_call | solution.py:286

commit v6 on v5

--- a/solution.py
+++ b/solution.py
@@ -16,7 +16,6 @@
 MESH = pl.DeviceIdType.MESH
 HALO = 24
 F32 = jnp.float32
-BF16 = jnp.bfloat16
 
 
 def green(coupling):
@@ -47,13 +46,8 @@
     return lax.broadcasted_iota(jnp.int32, shape, axis)
 
 
-def split(a):
-    high = a.astype(BF16)
-    return high, (a - high.astype(F32)).astype(BF16)
-
-
 def dot(a, b):
-    return jnp.dot(a, b, preferred_element_type=F32)
+    return jnp.dot(a, b, precision=lax.Precision.HIGHEST, preferred_element_type=F32)
 
 
 def kernel(
@@ -154,9 +148,9 @@
 
     load.start()
     distance = jnp.abs(iota((rows, rows), 0) - iota((rows, rows), 1))
-    across = [split(powers(c, distance)) for c in COUPLINGS]
+    across = [powers(c, distance) for c in COUPLINGS]
     distance = jnp.abs(iota((cols, cols), 0) - iota((cols, cols), 1))
-    along = [split(powers(c, distance)) for c in COUPLINGS]
+    along = [powers(c, distance) for c in COUPLINGS]
     edge = HALO + 8
     place = iota((edge, cols), 0)
     tail = iota((HALO, cols), 0)
@@ -178,13 +172,7 @@
     lane = iota((rows, 128), 1)
     source = iota((128, 128), 0)
     target = iota((128, 128), 1)
-    sides = [
-        [split(powers(c, jnp.abs(target - source + shift))) for c in COUPLINGS] for shift in (64, -64)
-    ]
-
-    def multiply(a, b):
-        ah, al = split(a)
-        return dot(ah, b[0]) + dot(al, b[0]) + dot(ah, b[1])
+    sides = [[powers(c, jnp.abs(target - source + shift)) for c in COUPLINGS] for shift in (64, -64)]
 
     load.wait()
     u = u_ref[...]
@@ -195,10 +183,9 @@
     col = iota((rows, cols), 1)
     inner = (row >= 2) & (row < rows - 2)
     for out, g, s in zip((dx_ref, dxx_ref), across, stencils(u, 0)):
-        high, low = split(jnp.where(inner, s, 0.0))
-        out[0] = dot(g[0], high) + dot(g[1], high) + dot(g[0], low)
+        out[0] = dot(g, jnp.where(inner, s, 0.0))
     inner = (col >= 2) & (col < cols - 2)
-    fy = [multiply(jnp.where(inner, s, 0.0), g) for g, s in zip(along, stencils(u, 1))]
+    fy = [dot(jnp.where(inner, s, 0.0), g) for g, s in zip(along, stencils(u, 1))]
 
     @pl.when(last)
     def _():
@@ -220,7 +207,7 @@
         low = jnp.where((lane >= 2) & (lane < 66), lower[k], 0.0)
         high = jnp.where((lane >= 62) & (lane < 126), upper[k], 0.0)
         out[0] = fy[k] + jnp.concatenate(
-            [multiply(low, sides[0][k]), multiply(high, sides[1][k])], axis=1
+            [dot(low, sides[0][k]), dot(high, sides[1][k])], axis=1
         )
 
     upper = stencils(jnp.concatenate([u[rows - 8 :], xr[...]], axis=0), 0)

time: 11.7 us -> 11.7 us (level)
  no operation moved by 1% of the time
where the time goes in v6:
time: 11.7 us; the launch traced here: 11.6 us
  Pallas kernels  11 us (94%)
  between operations  0.64 us (5%)
    pallas_call x1, Pallas kernels, local(): pl.pallas_call(functools.partial(kernel, nx, ny), out_shape=(pltpu.VMEM(v...  10.3 us
    pallas_call x1, Pallas kernels, local(): pl.pallas_call(finish, out_shape=(out,) * 4, in_specs=[vmem] * 6, out_spe...  0.7 us

profile of v6, /device:TPU:8, one launch (start us, length us, event | category | flops | bytes accessed | tf_op | source)
XLA Modules:
  0.0 11.6 jit_solution(1180983023082446983)
XLA Ops:
  0.6 10.3 %shard_map.46 = (f32[1,64,256]{2,1,0:T(8,128)S(1)}, f32[1,64,256]{2,1,0:T(8,128)S(1)}, f32[1,64,256]{2,1,0:T(8,128)S(1)}, f32[1,64,256]{2,1,0:T(8,128)S(1)}, f32...) custom-call(f32[1,64,256]{2,1,0:T(8,128)} %v_ref.1), custom_call_target="tpu_custom_call" | custom-call | tf_op jit(solution)/shard_map/pallas_call | solution.py:254
  10.9 0.7 %shard_map.47 = (f32[1,64,256]{2,1,0:T(8,128)}, f32[1,64,256]{2,1,0:T(8,128)}, f32[1,64,256]{2,1,0:T(8,128)}, f32[1,64,256]{2,1,0:T(8,128)}) custom-call(f32[1,64,256]{2,1,0:T(8,128)S(1)} %get-tuple-element.10.dx_in, f32[1,64,256]{2,1,0:T(8,128)S(1)} %get-tuple-element.11.dy_in, f32[1,64,256]{2,1,0:T(8,128)S(1)} %get-tuple-element.12.dxx_in, ...), custom_call_target="tpu_custom_call" | custom-call | tf_op jit(solution)/shard_map/pallas_call | solution.py:273

commit v7 on v6

--- a/solution.py
+++ b/solution.py
@@ -13,6 +13,7 @@
 SECOND_NEAR = 12.0 / 11.0
 SECOND_FAR = 3.0 / 44.0
 COUPLINGS = (1.0 / 3.0, 2.0 / 11.0)
+DIFFERENCES = ((FIRST_NEAR, FIRST_FAR, 1.0), (SECOND_NEAR, SECOND_FAR, -1.0))
 MESH = pl.DeviceIdType.MESH
 HALO = 24
 F32 = jnp.float32
@@ -65,10 +66,53 @@
     yl,
     yr,
     pool,
+    recv,
+    ready,
+):
+    pl.run_scoped(
+        functools.partial(
+            body,
+            nx,
+            ny,
+            v_ref,
+            dx_ref,
+            dy_ref,
+            dxx_ref,
+            dyy_ref,
+            edge_ref,
+            weight_ref,
+            u_ref,
+            xr,
+            yl,
+            yr,
+            pool,
+            recv,
+            ready,
+        ),
+        pltpu.SemaphoreType.DMA,
+        pltpu.SemaphoreType.DMA,
+    )
+
+
+def body(
+    nx,
+    ny,
+    v_ref,
+    dx_ref,
+    dy_ref,
+    dxx_ref,
+    dyy_ref,
+    edge_ref,
+    weight_ref,
+    u_ref,
+    xr,
+    yl,
+    yr,
+    pool,
+    recv,
+    ready,
     load_sem,
     send,
-    recv,
-    ready,
 ):
     ix = lax.axis_index("gx")
     iy = lax.axis_index("gy")
@@ -106,45 +150,46 @@
     to_left = remote(1, v_ref.at[0, :, pl.ds(0, 128)], yr, left)
 
     barrier = pltpu.get_barrier_semaphore()
-    signal(barrier, down)
+
+    def greet_sides():
+        signal(barrier, left)
+        signal(barrier, right)
+
+    def answer_sides():
+        signal(ready.at[0], right)
+        signal(ready.at[0], left)
+
+    @pl.when(jnp.logical_not(last))
+    def _():
+        signal(barrier, down)
+        pl.when(jnp.logical_not(before))(lambda: signal(barrier, up))
+        pl.when((odd == 1) & jnp.logical_not(before))(greet_sides)
+        pl.semaphore_wait(barrier, jnp.where(first, 1, 2) + 2 * (1 - odd))
+        to_up.start()
+
+        @pl.when(before)
+        def _():
+            signal(ready.at[0], up)
+            pl.when(odd == 0)(lambda: signal(ready.at[1], up))
+            pl.when(odd == 1)(greet_sides)
+
+        pl.when(jnp.logical_not(first))(lambda: to_down.start())
+        pl.when(odd == 0)(answer_sides)
+
+        @pl.when(odd == 1)
+        def _():
+            pl.semaphore_wait(ready.at[0], 2)
+            pl.when(before)(lambda: signal(ready.at[1], up))
+
+        to_right.start()
+        to_left.start()
 
     @pl.when(last)
     def _():
         pl.semaphore_wait(barrier, 1)
         to_up.start()
         signal(ready.at[1], up)
-
-    def greet_sides():
-        signal(barrier, left)
-        signal(barrier, right)
-
-    def answer_sides():
-        signal(ready.at[0], right)
-        signal(ready.at[0], left)
-
-    @pl.when(jnp.logical_not(last))
-    def _():
-        pl.when(jnp.logical_not(before))(lambda: signal(barrier, up))
-        pl.when((odd == 1) & jnp.logical_not(before))(greet_sides)
-        pl.semaphore_wait(barrier, jnp.where(first, 1, 2) + 2 * (1 - odd))
-        to_up.start()
-
-        @pl.when(before)
-        def _():
-            signal(ready.at[0], up)
-            pl.when(odd == 0)(lambda: signal(ready.at[1], up))
-            pl.when(odd == 1)(greet_sides)
-
-        pl.when(jnp.logical_not(first))(lambda: to_down.start())
-        pl.when(odd == 0)(answer_sides)
-
-        @pl.when(odd == 1)
-        def _():
-            pl.semaphore_wait(ready.at[0], 2)
-            pl.when(before)(lambda: signal(ready.at[1], up))
-
-        to_right.start()
-        to_left.start()
+        signal(barrier, down)
 
     load.start()
     distance = jnp.abs(iota((rows, rows), 0) - iota((rows, rows), 1))
@@ -157,9 +202,16 @@
     above = []
     for k, c in enumerate(COUPLINGS):
         _, scale = green(c)
-        weight_ref[k, pl.ds(0, edge), :] = (
-            jnp.where((place >= 2) & (place <= HALO), powers(c, jnp.abs(HALO - place)), 0.0) / scale
-        )
+        near, far, side = DIFFERENCES[k]
+        sum_weight = 0.0
+        row_weight = 0.0
+        for shift, factor in ((1, far), (0, near + far), (-1, side * (near + far)), (-2, side * far)):
+            at = place - shift
+            held = jnp.where((at >= 2) & (at <= HALO), powers(c, jnp.abs(HALO - at)), 0.0) / scale
+            sum_weight += factor * held
+            row_weight += jnp.where(at == HALO + 1, factor, 0.0)
+        weight_ref[k, pl.ds(0, edge), :] = sum_weight
+        weight_ref[k, pl.ds(edge + 2 * HALO, edge), :] = row_weight
         weight_ref[k, pl.ds(edge, HALO), :] = powers(c, tail)
         weight_ref[k, pl.ds(edge + HALO, HALO), :] = powers(c, jnp.abs(tail - 1))
         above.append(
@@ -216,8 +268,8 @@
         total = jnp.sum(weight * upper[k], axis=0, keepdims=True)
         out[0, pl.ds(rows - HALO, HALO), :] += far * total + close * upper[k][6:7]
 
+    take(rows + 2 * HALO, send)
     to_up.wait_recv()
-    take(rows + 2 * HALO, send)
 
 
 def finish(
@@ -234,13 +286,19 @@
         copy.start()
     edge = HALO + 8
     head = pl.ds(0, HALO)
-    lower = stencils(edge_ref[...], 0)
+    held = edge_ref[...]
+    steps = pltpu.roll(held, edge - 1, 0) - held
     for k, (part, out) in enumerate(((dx_in, dx_ref), (dxx_in, dxx_ref))):
-        total = jnp.sum(weight_ref[k, pl.ds(0, edge), :] * lower[k], axis=0, keepdims=True)
+        total = jnp.sum(weight_ref[k, pl.ds(0, edge), :] * steps, axis=0, keepdims=True)
+        source = jnp.sum(
+            weight_ref[k, pl.ds(edge + 3 * HALO - 8, 16), :] * steps[HALO - 8 : HALO + 8],
+            axis=0,
+            keepdims=True,
+        )
         low[k] = (
             part[0, head, :]
             + weight_ref[k, pl.ds(edge, HALO), :] * total
-            + weight_ref[k, pl.ds(edge + HALO, HALO), :] * lower[k][HALO + 1 : HALO + 2]
+            + weight_ref[k, pl.ds(edge + HALO, HALO), :] * source
         )
         pltpu.make_async_copy(low.at[k], out.at[0, head, :], sem).start()
     pltpu.make_async_copy(pool, pool, sem).wait()
@@ -254,7 +312,7 @@
     fields = pl.pallas_call(
         functools.partial(kernel, nx, ny),
         out_shape=(pltpu.VMEM(velocity.shape, F32),) * 4
-        + (pltpu.VMEM((HALO + 8, cols), F32), pltpu.VMEM((2, 3 * HALO + 8, cols), F32)),
+        + (pltpu.VMEM((HALO + 8, cols), F32), pltpu.VMEM((2, 4 * HALO + 16, cols), F32)),
         in_specs=[anywhere],
         out_specs=[vmem] * 6,
         scratch_shapes=[
@@ -263,8 +321,6 @@
             pltpu.VMEM((rows, 128), F32),
             pltpu.VMEM((rows, 128), F32),
             pltpu.VMEM((rows + 2 * HALO, cols), F32),
-            pltpu.SemaphoreType.DMA,
-            pltpu.SemaphoreType.DMA,
             pltpu.SemaphoreType.DMA((2,)),
             pltpu.SemaphoreType.REGULAR((2,)),
         ],

time: 11.7 us -> 11.7 us (level)
  no operation moved by 1% of the time
where the time goes in v7:
time: 11.7 us; the launch traced here: 11.6 us
  Pallas kernels  11 us (94%)
  between operations  0.64 us (5%)
    pallas_call x1, Pallas kernels, local(): pl.pallas_call(functools.partial(kernel, nx, ny), out_shape=(pltpu.VMEM(v...  10.3 us
    pallas_call x1, Pallas kernels, local(): pl.pallas_call(finish, out_shape=(out,) * 4, in_specs=[vmem] * 6, out_spe...  0.7 us

profile of v7, /device:TPU:8, one launch (start us, length us, event | category | flops | bytes accessed | tf_op | source)
XLA Modules:
  0.0 11.6 jit_solution(2884952715248904682)
XLA Ops:
  0.6 10.3 %shard_map.46 = (f32[1,64,256]{2,1,0:T(8,128)S(1)}, f32[1,64,256]{2,1,0:T(8,128)S(1)}, f32[1,64,256]{2,1,0:T(8,128)S(1)}, f32[1,64,256]{2,1,0:T(8,128)S(1)}, f32...) custom-call(f32[1,64,256]{2,1,0:T(8,128)} %v_ref.1), custom_call_target="tpu_custom_call" | custom-call | tf_op jit(solution)/shard_map/pallas_call | solution.py:312
  10.9 0.7 %shard_map.47 = (f32[1,64,256]{2,1,0:T(8,128)}, f32[1,64,256]{2,1,0:T(8,128)}, f32[1,64,256]{2,1,0:T(8,128)}, f32[1,64,256]{2,1,0:T(8,128)}) custom-call(f32[1,64,256]{2,1,0:T(8,128)S(1)} %get-tuple-element.10.dx_in, f32[1,64,256]{2,1,0:T(8,128)S(1)} %get-tuple-element.11.dy_in, f32[1,64,256]{2,1,0:T(8,128)S(1)} %get-tuple-element.12.dxx_in, ...), custom_call_target="tpu_custom_call" | custom-call | tf_op jit(solution)/shard_map/pallas_call | solution.py:329

commit v8 on v7

--- a/solution.py
+++ b/solution.py
@@ -124,7 +124,7 @@
     first = ix == 0
     last = ix == nx - 1
     before = ix == nx - 2
-    odd = lax.rem(iy, 2)
+    odd = jnp.bitwise_and(iy, 1)
 
     def signal(semaphore, other):
         pl.semaphore_signal(semaphore, inc=1, device_id=other, device_id_type=MESH)
@@ -187,8 +187,13 @@
     @pl.when(last)
     def _():
         pl.semaphore_wait(barrier, 1)
-        to_up.start()
-        signal(ready.at[1], up)
+        remote(
+            0,
+            v_ref.at[0, pl.ds(rows - HALO, HALO), :],
+            edge_ref.at[pl.ds(0, HALO), :],
+            {"gx": 0},
+        ).start()
+        signal(ready.at[1], {"gx": 0})
         signal(barrier, down)
 
     load.start()

time: 11.7 us -> 11.7 us (level)
  no operation moved by 1% of the time
where the time goes in v8:
time: 11.7 us; the launch traced here: 11.6 us
  Pallas kernels  11 us (94%)
  between operations  0.64 us (5%)
    pallas_call x1, Pallas kernels, local(): pl.pallas_call(functools.partial(kernel, nx, ny), out_shape=(pltpu.VMEM(v...  10.3 us
    pallas_call x1, Pallas kernels, local(): pl.pallas_call(finish, out_shape=(out,) * 4, in_specs=[vmem] * 6, out_spe...  0.7 us

profile of v8, /device:TPU:8, one launch (start us, length us, event | category | flops | bytes accessed | tf_op | source)
XLA Modules:
  0.0 11.6 jit_solution(17964701512101108091)
XLA Ops:
  0.6 10.3 %shard_map.46 = (f32[1,64,256]{2,1,0:T(8,128)S(1)}, f32[1,64,256]{2,1,0:T(8,128)S(1)}, f32[1,64,256]{2,1,0:T(8,128)S(1)}, f32[1,64,256]{2,1,0:T(8,128)S(1)}, f32...) custom-call(f32[1,64,256]{2,1,0:T(8,128)} %v_ref.1), custom_call_target="tpu_custom_call" | custom-call | tf_op jit(solution)/shard_map/pallas_call | solution.py:317
  10.9 0.7 %shard_map.47 = (f32[1,64,256]{2,1,0:T(8,128)}, f32[1,64,256]{2,1,0:T(8,128)}, f32[1,64,256]{2,1,0:T(8,128)}, f32[1,64,256]{2,1,0:T(8,128)}) custom-call(f32[1,64,256]{2,1,0:T(8,128)S(1)} %get-tuple-element.10.dx_in, f32[1,64,256]{2,1,0:T(8,128)S(1)} %get-tuple-element.11.dy_in, f32[1,64,256]{2,1,0:T(8,128)S(1)} %get-tuple-element.12.dxx_in, ...), custom_call_target="tpu_custom_call" | custom-call | tf_op jit(solution)/shard_map/pallas_call | solution.py:334

commit v9 on v7

--- a/solution.py
+++ b/solution.py
@@ -276,14 +276,17 @@
     dx_in, dy_in, dxx_in, dyy_in, edge_ref, weight_ref, dx_ref, dy_ref, dxx_ref, dyy_ref, low, pool, sem
 ):
     rest = pl.ds(HALO, dx_in.shape[1] - HALO)
-    copies = [
-        pltpu.make_async_copy(dy_in, dy_ref, sem),
-        pltpu.make_async_copy(dyy_in, dyy_ref, sem),
-        pltpu.make_async_copy(dx_in.at[0, rest, :], dx_ref.at[0, rest, :], sem),
-        pltpu.make_async_copy(dxx_in.at[0, rest, :], dxx_ref.at[0, rest, :], sem),
-    ]
-    for copy in copies:
-        copy.start()
+    half = pl.ds(0, dx_in.shape[1] // 2)
+    other = pl.ds(dx_in.shape[1] // 2, dx_in.shape[1] // 2)
+    for part, out, place in (
+        (dy_in, dy_ref, half),
+        (dyy_in, dyy_ref, half),
+        (dx_in, dx_ref, rest),
+        (dxx_in, dxx_ref, rest),
+        (dy_in, dy_ref, other),
+        (dyy_in, dyy_ref, other),
+    ):
+        pltpu.make_async_copy(part.at[0, place, :], out.at[0, place, :], sem).start()
     edge = HALO + 8
     head = pl.ds(0, HALO)
     held = edge_ref[...]

time: 11.7 us -> 11.7 us (level)
  no operation moved by 1% of the time
where the time goes in v9:
time: 11.7 us; the launch traced here: 11.6 us
  Pallas kernels  11 us (94%)
  between operations  0.64 us (5%)
    pallas_call x1, Pallas kernels, local(): pl.pallas_call(functools.partial(kernel, nx, ny), out_shape=(pltpu.VMEM(v...  10.3 us
    pallas_call x1, Pallas kernels, local(): pl.pallas_call(finish, out_shape=(out,) * 4, in_specs=[vmem] * 6, out_spe...  0.7 us

profile of v9, /device:TPU:8, one launch (start us, length us, event | category | flops | bytes accessed | tf_op | source)
XLA Modules:
  0.0 11.6 jit_solution(11619346801633964903)
XLA Ops:
  0.6 10.3 %shard_map.46 = (f32[1,64,256]{2,1,0:T(8,128)S(1)}, f32[1,64,256]{2,1,0:T(8,128)S(1)}, f32[1,64,256]{2,1,0:T(8,128)S(1)}, f32[1,64,256]{2,1,0:T(8,128)S(1)}, f32...) custom-call(f32[1,64,256]{2,1,0:T(8,128)} %v_ref.1), custom_call_target="tpu_custom_call" | custom-call | tf_op jit(solution)/shard_map/pallas_call | solution.py:315
  10.9 0.7 %shard_map.47 = (f32[1,64,256]{2,1,0:T(8,128)}, f32[1,64,256]{2,1,0:T(8,128)}, f32[1,64,256]{2,1,0:T(8,128)}, f32[1,64,256]{2,1,0:T(8,128)}) custom-call(f32[1,64,256]{2,1,0:T(8,128)S(1)} %get-tuple-element.10.dx_in, f32[1,64,256]{2,1,0:T(8,128)S(1)} %get-tuple-element.11.dy_in, f32[1,64,256]{2,1,0:T(8,128)S(1)} %get-tuple-element.12.dxx_in, ...), custom_call_target="tpu_custom_call" | custom-call | tf_op jit(solution)/shard_map/pallas_call | solution.py:332

commit v10 on v9

--- a/solution.py
+++ b/solution.py
@@ -124,7 +124,7 @@
     first = ix == 0
     last = ix == nx - 1
     before = ix == nx - 2
-    odd = lax.rem(iy, 2)
+    odd = jnp.bitwise_and(iy, 1)
 
     def signal(semaphore, other):
         pl.semaphore_signal(semaphore, inc=1, device_id=other, device_id_type=MESH)
@@ -187,8 +187,13 @@
     @pl.when(last)
     def _():
         pl.semaphore_wait(barrier, 1)
-        to_up.start()
-        signal(ready.at[1], up)
+        remote(
+            0,
+            v_ref.at[0, pl.ds(rows - HALO, HALO), :],
+            edge_ref.at[pl.ds(0, HALO), :],
+            {"gx": 0},
+        ).start()
+        signal(ready.at[1], {"gx": 0})
         signal(barrier, down)
 
     load.start()

time: 11.7 us -> 11.7 us (level)
  no operation moved by 1% of the time
where the time goes in v10:
time: 11.7 us; the launch traced here: 11.6 us
  Pallas kernels  11 us (94%)
  between operations  0.64 us (5%)
    pallas_call x1, Pallas kernels, local(): pl.pallas_call(functools.partial(kernel, nx, ny), out_shape=(pltpu.VMEM(v...  10.3 us
    pallas_call x1, Pallas kernels, local(): pl.pallas_call(finish, out_shape=(out,) * 4, in_specs=[vmem] * 6, out_spe...  0.7 us

profile of v10, /device:TPU:8, one launch (start us, length us, event | category | flops | bytes accessed | tf_op | source)
XLA Modules:
  0.0 11.6 jit_solution(810446941146748005)
XLA Ops:
  0.6 10.3 %shard_map.46 = (f32[1,64,256]{2,1,0:T(8,128)S(1)}, f32[1,64,256]{2,1,0:T(8,128)S(1)}, f32[1,64,256]{2,1,0:T(8,128)S(1)}, f32[1,64,256]{2,1,0:T(8,128)S(1)}, f32...) custom-call(f32[1,64,256]{2,1,0:T(8,128)} %v_ref.1), custom_call_target="tpu_custom_call" | custom-call | tf_op jit(solution)/shard_map/pallas_call | solution.py:320
  10.9 0.7 %shard_map.47 = (f32[1,64,256]{2,1,0:T(8,128)}, f32[1,64,256]{2,1,0:T(8,128)}, f32[1,64,256]{2,1,0:T(8,128)}, f32[1,64,256]{2,1,0:T(8,128)}) custom-call(f32[1,64,256]{2,1,0:T(8,128)S(1)} %get-tuple-element.10.dx_in, f32[1,64,256]{2,1,0:T(8,128)S(1)} %get-tuple-element.11.dy_in, f32[1,64,256]{2,1,0:T(8,128)S(1)} %get-tuple-element.12.dxx_in, ...), custom_call_target="tpu_custom_call" | custom-call | tf_op jit(solution)/shard_map/pallas_call | solution.py:337
